TPU v7x, 32 devices: a whole 2x2x4 slice. The times are simulated.
32 devices in a mesh: uly: 8 (over z, y), blk: 4 (over x, core).
Axes of the slice: x: 2, y: 2, z: 4, core: 2. Of those that a mesh axis runs over, the one named last changes fastest.
Arguments:
- queries: bfloat16 [2048, 2048], P(('blk', 'uly')), may hold values from -20 to 20
- keys: bfloat16 [2048, 2048], P(('blk', 'uly')), may hold values from -20 to 20
- values: bfloat16 [2048, 2048], P(('blk', 'uly')), may hold values from -6 to 6
- block_list: int32 [32, 16, 16], P('uly', 'blk'), may hold values from -1 to 15, as said below
Outputs:
- attended: bfloat16 [2048, 2048], P(('blk', 'uly'))
Inputs may be any that keep to these rules, and one draw needn't show every extreme that they name: block_list[h, b, 0] = b; every other entry is -1 (an empty slot) or a block below b, and the blocks named in one list are distinct.
All inputs are finite; a program needn't handle non-finite values.
Results may differ from a plain program's by a relative error of at most 0.0045.
Values may be sent and summed in bfloat16 or wider, within the bound.
No kernel may reach another device: no remote copies, remote signals or barrier semaphores. Data moves between devices by JAX's collectives and lax.ppermute only.
A program may use at most 64 MiB of HBM per device.

v0:
```python
import jax
import jax.numpy as jnp
from jax import lax
from jax.sharding import PartitionSpec as P

BLOCK = 128
QGROUP = 2


def head_major(token_rows, heads_local, head_dim):
    return token_rows.reshape(token_rows.shape[0] // BLOCK, BLOCK, heads_local, head_dim).transpose(
        2, 0, 1, 3
    )


def select_blocks(source, chosen):
    return jnp.take(source, chosen, axis=0)


def attend_block(operand):
    query_group, key_slots, value_slots, chosen, query_block = operand
    scale = query_group.shape[-1] ** (-0.5)
    scores = (
        jnp.einsum("abd,asjd->absj", query_group, key_slots, preferred_element_type=jnp.float32)
        * scale
    )
    positions = jnp.arange(BLOCK, dtype=jnp.int32)
    query_pos = query_block[:, None] * BLOCK + positions[None, :]
    key_pos = jnp.maximum(chosen, 0)[:, :, None] * BLOCK + positions[None, None, :]
    allowed = (chosen[:, None, :, None] >= 0) & (
        key_pos[:, None, :, :] <= query_pos[:, :, None, None]
    )
    scores = jnp.where(allowed, scores, -1e30)
    row_max = jnp.max(scores, axis=(2, 3), keepdims=True)
    weights = jnp.where(allowed, jnp.exp(scores - row_max), 0.0)
    denominator = jnp.sum(weights, axis=(2, 3))
    rounded = weights.astype(jnp.bfloat16)
    summed = jnp.einsum("absj,asjd->abd", rounded, value_slots, preferred_element_type=jnp.float32)
    return (summed / denominator[:, :, None]).astype(jnp.bfloat16)


def local(queries, keys, values, block_list):
    heads_local = block_list.shape[0]
    blocks_dev = block_list.shape[1]
    slot_count = block_list.shape[2]
    head_dim = queries.shape[1] // (heads_local * lax.axis_size("uly"))
    first_block = lax.axis_index("blk") * blocks_dev
    query_rows, key_rows, value_rows = (
        lax.all_to_all(queries, "uly", split_axis=1, concat_axis=0, tiled=True),
        lax.all_to_all(keys, "uly", split_axis=1, concat_axis=0, tiled=True),
        lax.all_to_all(values, "uly", split_axis=1, concat_axis=0, tiled=True),
    )
    keys_all = lax.all_gather(key_rows, "blk", axis=0, tiled=True)
    values_all = lax.all_gather(value_rows, "blk", axis=0, tiled=True)
    chosen = jnp.maximum(block_list, 0)
    key_slots = jax.vmap(select_blocks)(head_major(keys_all, heads_local, head_dim), chosen)
    value_slots = jax.vmap(select_blocks)(head_major(values_all, heads_local, head_dim), chosen)
    key_slots, value_slots = (key_slots, value_slots)
    groups = heads_local * blocks_dev // QGROUP
    query_heads = head_major(query_rows, heads_local, head_dim).reshape(
        groups, QGROUP, BLOCK, head_dim
    )
    key_groups = key_slots.reshape(groups, QGROUP, slot_count, BLOCK, head_dim)
    value_groups = value_slots.reshape(groups, QGROUP, slot_count, BLOCK, head_dim)
    list_groups = block_list.reshape(groups, QGROUP, slot_count)
    block_numbers = first_block + jnp.arange(blocks_dev, dtype=jnp.int32)
    block_groups = jnp.broadcast_to(block_numbers[None, :], (heads_local, blocks_dev)).reshape(
        groups, QGROUP
    )
    result = lax.map(
        attend_block, (query_heads, key_groups, value_groups, list_groups, block_groups)
    )
    result = result.reshape(heads_local, blocks_dev * BLOCK, head_dim).transpose(1, 0, 2)
    result = result.reshape(blocks_dev * BLOCK, heads_local * head_dim)
    return lax.all_to_all(result, "uly", split_axis=0, concat_axis=1, tiled=True)


def solution(mesh):
    placed = (
        P(("blk", "uly"), None),
        P(("blk", "uly"), None),
        P(("blk", "uly"), None),
        P("uly", "blk", None),
    )
    return jax.shard_map(
        local, mesh=mesh, in_specs=placed, out_specs=P(("blk", "uly"), None), check_vma=False
    )
```

profile of v0, /device:TPU:0, one launch (start us, length us, event | category | flops | bytes accessed | tf_op | source)
XLA Modules:
  0.0 148.7 jit_solution(14057702400680355051)
XLA Ops:
  6.5 1.0 copy.82
  7.6 16.1 %all_to_all.73 = bf16[64,8,256]{2,0,1:T(8,128)(2,1)} all-to-all(bf16[64,8,256]{2,0,1:T(8,128)(2,1)S(1)} %bitcast.102), channel_id=1, replica_groups=mesh['uly'=8,'blk'=4] {'uly'}, dimensions={1} | all-to-all | bytes 524288 | tf_op jit(solution)/shard_map/all_to_all | solution.py:50
  23.8 1.0 copy.81
  24.7 12.1 %all_to_all.74 = bf16[64,8,256]{2,0,1:T(8,128)(2,1)} all-to-all(bf16[64,8,256]{2,0,1:T(8,128)(2,1)S(1)} %bitcast.103), channel_id=1, replica_groups=mesh['uly'=8,'blk'=4] {'uly'}, dimensions={1} | all-to-all | bytes 524288 | tf_op jit(solution)/shard_map/all_to_all | solution.py:51
  37.5 3.6 %all-to-all-start = ((bf16[64,8,256]{2,0,1:T(8,128)(2,1)}), bf16[64,8,256]{2,0,1:T(8,128)(2,1)S(1)}, u32[]{:S(2)}, u32[]{:S(2)}) async-start(bf16[64,8,256]{2,0,1:T(8,128)(2,1)} %bitcast.73), calls=%async_computation | async-start | bytes 524288 | tf_op jit(solution)/shard_map/all_to_all | solution.py:49
  41.3 8.3 %all-to-all-done = bf16[64,8,256]{2,0,1:T(8,128)(2,1)S(1)} async-done(((bf16[64,8,256]{2,0,1:T(8,128)(2,1)}), bf16[64,8,256]{2,0,1:T(8,128)(2,1)S(1)}, u32[]{:S(2)}, u32[]{:S(2)}) %all-to-all-start) | async-done | bytes 262176 | tf_op jit(solution)/shard_map/all_to_all | solution.py:49
  50.3 3.3 %reshape.151 = bf16[16,128,4,64]{3,2,1,0:T(4,128)(2,1)S(1)} reshape(bf16[2048,256]{1,0:T(8,128)(2,1)} %all-gather.3.cloned.1.call-done) | data formatting | bytes 2097152 | tf_op jit(solution)/shard_map/reshape | solution.py:11
  53.6 1.4 copy.49
  55.0 2.8 %all-gather.5.cloned.1.call-done = bf16[2048,256]{1,0:T(8,128)(2,1)} async-done(((bf16[512,256]{1,0:T(8,128)(2,1)}), bf16[2048,256]{1,0:T(8,128)(2,1)}) %all-gather.5.cloned.1.call-update) | async-done | bytes 1048592 | tf_op jit(solution)/shard_map/all_gather | solution.py:54
  57.9 4.4 %reshape.152 = bf16[16,128,4,64]{3,2,1,0:T(4,128)(2,1)} reshape(bf16[2048,256]{1,0:T(8,128)(2,1)} %all-gather.5.cloned.1.call-done) | data formatting | bytes 2097152 | tf_op jit(solution)/shard_map/reshape | solution.py:11
  62.3 3.0 %copy.52 = bf16[16,128,4,64]{1,3,0,2:T(8,128)(2,1)S(1)} copy(bf16[16,128,4,64]{3,2,1,0:T(4,128)(2,1)} %reshape.152) | data formatting | bytes 2097152 | tf_op jit(solution)/shard_map/reshape | solution.py:11
  65.3 3.3 %gather_fusion = bf16[256,128,64]{1,2,0:T(8,128)(2,1)} fusion(bf16[4,16,128,64]{2,3,1,0:T(8,128)(2,1)S(1)} %bitcast.90, s32[256]{0:T(256)S(1)} %reshape.139), kind=kCustom, calls=%fused_computation.clone | custom fusion | bytes 8390656 | tf_op jit(solution)/shard_map/vmap(jit(_take))/gather | solution.py:17
  68.6 3.3 %gather_fusion.1 = bf16[256,128,64]{1,2,0:T(8,128)(2,1)} fusion(bf16[4,16,128,64]{2,3,1,0:T(8,128)(2,1)S(1)} %bitcast.91, s32[256]{0:T(256)S(1)} %reshape.139), kind=kCustom, calls=%fused_computation.1.clone | custom fusion | bytes 8390656 | tf_op jit(solution)/shard_map/vmap(jit(_take))/gather | solution.py:17
  72.0 5.9 %broadcast_select_fusion = (bf16[4,4,16,128,64]{3,4,2,1,0:T(8,128)(2,1)}, bf16[4,4,16,128,64]{3,4,2,1,0:T(8,128)(2,1)}) fusion(bf16[4,4,16,128,64]{3,4,2,1,0:T(8,128)(2,1)} %bitcast.93, pred[4,4,16]{2,1,0:T(4,128)(4,1)S(1)} %maximum_compare_fusion, bf16[4,4,16,128,64]{3,4,2,1,0:T(8,128)(2,1)} %bitcast.92), kind=kLoop, calls=%fused_computation.33 | loop fusion | flops 4194304 | bytes 16777472 | tf_op jit(solution)/shard_map/vmap(jit(_take))/select_n | solution.py:17
  77.9 47.7 %while.10 = (s32[]{:T(128)}, bf16[8,2,128,64]{2,1,0,3:T(2,128)(2,1)S(1)}, s32[8,2,16]{2,1,0:T(2,128)S(1)}, s32[8,2]{1,0:T(8,128)S(1)}, bf16[8,2,128,64]{2,3,1,0:...) while((s32[]{:T(128)}, ...), condition=%wide.region_3.5_spmd, body=%wide.region_0.4_spmd.sunk | while | flops 142118752 | bytes 7548637 | solution.py:70
  78.1 2.9 %fusion.31 = (f32[2,128]{1,0:T(2,128)S(1)}, f32[2,128,16,128]{1,3,2,0:T(8,128)S(1)}) fusion(bf16[8,2,16,128,64]{3,4,2,1,0:T(8,128)(2,1)} %get-tuple-element.165, s32[]{:T(128)} %get-tuple-element.152, bf16[8,2,128,64]{2,3,1,0:T(8,128)(2,1)S(1)} %get-tuple-element.164, s32[2,128]{1,0:T(2,128)S(1)} %iota_add_fusion.4, ...), kind=kOutput, calls=%fused_computation.41.clone.1 | convolution fusion | flops 69730048 | bytes 2674176 | tf_op jit(solution)/shard_map/while/body/eval_jaxpr/abd,asjd->absj/dot_general | solution.py:24
  81.8 2.1 %fusion.33 = bf16[1,2,128,64]{2,3,1,0:T(8,128)(2,1)S(1)} fusion(f32[2,128,16,128]{1,3,2,0:T(8,128)S(1)} %get-tuple-element.142, f32[2,128]{1,0:T(2,128)S(1)} %get-tuple-element.143, s32[2,128]{1,0:T(2,128)S(1)} %iota_add_fusion.4, s32[2,16,128]{2,1,0:T(8,128)S(1)} %iota_add_fusion.5, pred[2,16]{1,0:T(4,128)(4,1)S(1)} %compare_bitcast_fusion.2, ...), kind=kOutput, calls=%fused_computation.10.clone.1 | convolution fusion | flops 69763072 | bytes 2674208 | tf_op jit(solution)/shard_map/while/body/eval_jaxpr/absj,asjd->abd/dot_general | solution.py:38
  84.1 2.9 %fusion.31 = (f32[2,128]{1,0:T(2,128)S(1)}, f32[2,128,16,128]{1,3,2,0:T(8,128)S(1)}) fusion(bf16[8,2,16,128,64]{3,4,2,1,0:T(8,128)(2,1)} %get-tuple-element.165, s32[]{:T(128)} %get-tuple-element.152, bf16[8,2,128,64]{2,3,1,0:T(8,128)(2,1)S(1)} %get-tuple-element.164, s32[2,128]{1,0:T(2,128)S(1)} %iota_add_fusion.4, ...), kind=kOutput, calls=%fused_computation.41.clone.1 | convolution fusion | flops 69730048 | bytes 2674176 | tf_op jit(solution)/shard_map/while/body/eval_jaxpr/abd,asjd->absj/dot_general | solution.py:24
  87.7 2.1 %fusion.33 = bf16[1,2,128,64]{2,3,1,0:T(8,128)(2,1)S(1)} fusion(f32[2,128,16,128]{1,3,2,0:T(8,128)S(1)} %get-tuple-element.142, f32[2,128]{1,0:T(2,128)S(1)} %get-tuple-element.143, s32[2,128]{1,0:T(2,128)S(1)} %iota_add_fusion.4, s32[2,16,128]{2,1,0:T(8,128)S(1)} %iota_add_fusion.5, pred[2,16]{1,0:T(4,128)(4,1)S(1)} %compare_bitcast_fusion.2, ...), kind=kOutput, calls=%fused_computation.10.clone.1 | convolution fusion | flops 69763072 | bytes 2674208 | tf_op jit(solution)/shard_map/while/body/eval_jaxpr/absj,asjd->abd/dot_general | solution.py:38
  90.1 2.9 %fusion.31 = (f32[2,128]{1,0:T(2,128)S(1)}, f32[2,128,16,128]{1,3,2,0:T(8,128)S(1)}) fusion(bf16[8,2,16,128,64]{3,4,2,1,0:T(8,128)(2,1)} %get-tuple-element.165, s32[]{:T(128)} %get-tuple-element.152, bf16[8,2,128,64]{2,3,1,0:T(8,128)(2,1)S(1)} %get-tuple-element.164, s32[2,128]{1,0:T(2,128)S(1)} %iota_add_fusion.4, ...), kind=kOutput, calls=%fused_computation.41.clone.1 | convolution fusion | flops 69730048 | bytes 2674176 | tf_op jit(solution)/shard_map/while/body/eval_jaxpr/abd,asjd->absj/dot_general | solution.py:24
  93.7 2.1 %fusion.33 = bf16[1,2,128,64]{2,3,1,0:T(8,128)(2,1)S(1)} fusion(f32[2,128,16,128]{1,3,2,0:T(8,128)S(1)} %get-tuple-element.142, f32[2,128]{1,0:T(2,128)S(1)} %get-tuple-element.143, s32[2,128]{1,0:T(2,128)S(1)} %iota_add_fusion.4, s32[2,16,128]{2,1,0:T(8,128)S(1)} %iota_add_fusion.5, pred[2,16]{1,0:T(4,128)(4,1)S(1)} %compare_bitcast_fusion.2, ...), kind=kOutput, calls=%fused_computation.10.clone.1 | convolution fusion | flops 69763072 | bytes 2674208 | tf_op jit(solution)/shard_map/while/body/eval_jaxpr/absj,asjd->abd/dot_general | solution.py:38
  96.0 2.9 %fusion.31 = (f32[2,128]{1,0:T(2,128)S(1)}, f32[2,128,16,128]{1,3,2,0:T(8,128)S(1)}) fusion(bf16[8,2,16,128,64]{3,4,2,1,0:T(8,128)(2,1)} %get-tuple-element.165, s32[]{:T(128)} %get-tuple-element.152, bf16[8,2,128,64]{2,3,1,0:T(8,128)(2,1)S(1)} %get-tuple-element.164, s32[2,128]{1,0:T(2,128)S(1)} %iota_add_fusion.4, ...), kind=kOutput, calls=%fused_computation.41.clone.1 | convolution fusion | flops 69730048 | bytes 2674176 | tf_op jit(solution)/shard_map/while/body/eval_jaxpr/abd,asjd->absj/dot_general | solution.py:24
  99.7 2.1 %fusion.33 = bf16[1,2,128,64]{2,3,1,0:T(8,128)(2,1)S(1)} fusion(f32[2,128,16,128]{1,3,2,0:T(8,128)S(1)} %get-tuple-element.142, f32[2,128]{1,0:T(2,128)S(1)} %get-tuple-element.143, s32[2,128]{1,0:T(2,128)S(1)} %iota_add_fusion.4, s32[2,16,128]{2,1,0:T(8,128)S(1)} %iota_add_fusion.5, pred[2,16]{1,0:T(4,128)(4,1)S(1)} %compare_bitcast_fusion.2, ...), kind=kOutput, calls=%fused_computation.10.clone.1 | convolution fusion | flops 69763072 | bytes 2674208 | tf_op jit(solution)/shard_map/while/body/eval_jaxpr/absj,asjd->abd/dot_general | solution.py:38
  102.0 2.9 %fusion.31 = (f32[2,128]{1,0:T(2,128)S(1)}, f32[2,128,16,128]{1,3,2,0:T(8,128)S(1)}) fusion(bf16[8,2,16,128,64]{3,4,2,1,0:T(8,128)(2,1)} %get-tuple-element.165, s32[]{:T(128)} %get-tuple-element.152, bf16[8,2,128,64]{2,3,1,0:T(8,128)(2,1)S(1)} %get-tuple-element.164, s32[2,128]{1,0:T(2,128)S(1)} %iota_add_fusion.4, ...), kind=kOutput, calls=%fused_computation.41.clone.1 | convolution fusion | flops 69730048 | bytes 2674176 | tf_op jit(solution)/shard_map/while/body/eval_jaxpr/abd,asjd->absj/dot_general | solution.py:24
  105.6 2.1 %fusion.33 = bf16[1,2,128,64]{2,3,1,0:T(8,128)(2,1)S(1)} fusion(f32[2,128,16,128]{1,3,2,0:T(8,128)S(1)} %get-tuple-element.142, f32[2,128]{1,0:T(2,128)S(1)} %get-tuple-element.143, s32[2,128]{1,0:T(2,128)S(1)} %iota_add_fusion.4, s32[2,16,128]{2,1,0:T(8,128)S(1)} %iota_add_fusion.5, pred[2,16]{1,0:T(4,128)(4,1)S(1)} %compare_bitcast_fusion.2, ...), kind=kOutput, calls=%fused_computation.10.clone.1 | convolution fusion | flops 69763072 | bytes 2674208 | tf_op jit(solution)/shard_map/while/body/eval_jaxpr/absj,asjd->abd/dot_general | solution.py:38
  108.0 2.9 %fusion.31 = (f32[2,128]{1,0:T(2,128)S(1)}, f32[2,128,16,128]{1,3,2,0:T(8,128)S(1)}) fusion(bf16[8,2,16,128,64]{3,4,2,1,0:T(8,128)(2,1)} %get-tuple-element.165, s32[]{:T(128)} %get-tuple-element.152, bf16[8,2,128,64]{2,3,1,0:T(8,128)(2,1)S(1)} %get-tuple-element.164, s32[2,128]{1,0:T(2,128)S(1)} %iota_add_fusion.4, ...), kind=kOutput, calls=%fused_computation.41.clone.1 | convolution fusion | flops 69730048 | bytes 2674176 | tf_op jit(solution)/shard_map/while/body/eval_jaxpr/abd,asjd->absj/dot_general | solution.py:24
  111.6 2.1 %fusion.33 = bf16[1,2,128,64]{2,3,1,0:T(8,128)(2,1)S(1)} fusion(f32[2,128,16,128]{1,3,2,0:T(8,128)S(1)} %get-tuple-element.142, f32[2,128]{1,0:T(2,128)S(1)} %get-tuple-element.143, s32[2,128]{1,0:T(2,128)S(1)} %iota_add_fusion.4, s32[2,16,128]{2,1,0:T(8,128)S(1)} %iota_add_fusion.5, pred[2,16]{1,0:T(4,128)(4,1)S(1)} %compare_bitcast_fusion.2, ...), kind=kOutput, calls=%fused_computation.10.clone.1 | convolution fusion | flops 69763072 | bytes 2674208 | tf_op jit(solution)/shard_map/while/body/eval_jaxpr/absj,asjd->abd/dot_general | solution.py:38
  113.9 2.9 %fusion.31 = (f32[2,128]{1,0:T(2,128)S(1)}, f32[2,128,16,128]{1,3,2,0:T(8,128)S(1)}) fusion(bf16[8,2,16,128,64]{3,4,2,1,0:T(8,128)(2,1)} %get-tuple-element.165, s32[]{:T(128)} %get-tuple-element.152, bf16[8,2,128,64]{2,3,1,0:T(8,128)(2,1)S(1)} %get-tuple-element.164, s32[2,128]{1,0:T(2,128)S(1)} %iota_add_fusion.4, ...), kind=kOutput, calls=%fused_computation.41.clone.1 | convolution fusion | flops 69730048 | bytes 2674176 | tf_op jit(solution)/shard_map/while/body/eval_jaxpr/abd,asjd->absj/dot_general | solution.py:24
  117.6 2.1 %fusion.33 = bf16[1,2,128,64]{2,3,1,0:T(8,128)(2,1)S(1)} fusion(f32[2,128,16,128]{1,3,2,0:T(8,128)S(1)} %get-tuple-element.142, f32[2,128]{1,0:T(2,128)S(1)} %get-tuple-element.143, s32[2,128]{1,0:T(2,128)S(1)} %iota_add_fusion.4, s32[2,16,128]{2,1,0:T(8,128)S(1)} %iota_add_fusion.5, pred[2,16]{1,0:T(4,128)(4,1)S(1)} %compare_bitcast_fusion.2, ...), kind=kOutput, calls=%fused_computation.10.clone.1 | convolution fusion | flops 69763072 | bytes 2674208 | tf_op jit(solution)/shard_map/while/body/eval_jaxpr/absj,asjd->abd/dot_general | solution.py:38
  119.9 2.9 %fusion.31 = (f32[2,128]{1,0:T(2,128)S(1)}, f32[2,128,16,128]{1,3,2,0:T(8,128)S(1)}) fusion(bf16[8,2,16,128,64]{3,4,2,1,0:T(8,128)(2,1)} %get-tuple-element.165, s32[]{:T(128)} %get-tuple-element.152, bf16[8,2,128,64]{2,3,1,0:T(8,128)(2,1)S(1)} %get-tuple-element.164, s32[2,128]{1,0:T(2,128)S(1)} %iota_add_fusion.4, ...), kind=kOutput, calls=%fused_computation.41.clone.1 | convolution fusion | flops 69730048 | bytes 2674176 | tf_op jit(solution)/shard_map/while/body/eval_jaxpr/abd,asjd->absj/dot_general | solution.py:24
  123.5 2.1 %fusion.33 = bf16[1,2,128,64]{2,3,1,0:T(8,128)(2,1)S(1)} fusion(f32[2,128,16,128]{1,3,2,0:T(8,128)S(1)} %get-tuple-element.142, f32[2,128]{1,0:T(2,128)S(1)} %get-tuple-element.143, s32[2,128]{1,0:T(2,128)S(1)} %iota_add_fusion.4, s32[2,16,128]{2,1,0:T(8,128)S(1)} %iota_add_fusion.5, pred[2,16]{1,0:T(4,128)(4,1)S(1)} %compare_bitcast_fusion.2, ...), kind=kOutput, calls=%fused_computation.10.clone.1 | convolution fusion | flops 69763072 | bytes 2674208 | tf_op jit(solution)/shard_map/while/body/eval_jaxpr/absj,asjd->abd/dot_general | solution.py:38
  126.5 14.6 %all_to_all.75 = bf16[8,64,256]{2,1,0:T(8,128)(2,1)S(1)} all-to-all(bf16[8,64,256]{2,1,0:T(8,128)(2,1)S(1)} %reshape.153), channel_id=1, replica_groups=mesh['uly'=8,'blk'=4] {'uly'}, dimensions={0} | all-to-all | bytes 524288 | tf_op jit(solution)/shard_map/all_to_all | solution.py:75
  (81 shorter events, 11.2 us)
Async XLA Ops:
  6.5 30.3 %copy-start = (bf16[64,2048]{1,0:T(8,128)(2,1)S(1)}, bf16[64,2048]{1,0:T(8,128)(2,1)}, u32[]{:S(2)}) copy-start(bf16[64,2048]{1,0:T(8,128)(2,1)} %param.8) | copy-start | bytes 786436
  6.5 34.6 %copy-start.2 = (s32[4,4,16]{2,1,0:T(4,128)S(1)}, s32[4,4,16]{2,1,0:T(4,128)}, u32[]{:S(2)}) copy-start(s32[4,4,16]{2,1,0:T(4,128)} %param.11) | copy-start | bytes 3076
  6.5 43.7 %all-gather.3.cloned.1.call-start = ((), (), s32[]{:S(2)}) async-start(), calls=%async_computation.4 | async-start | bytes 1310720 | tf_op jit(solution)/shard_map/all_gather | solution.py:53
  23.7 34.1 %all-gather.5.cloned.1.call-start = ((), (), s32[]{:S(2)}) async-start(), calls=%async_computation.5 | async-start | bytes 1310720 | tf_op jit(solution)/shard_map/all_gather | solution.py:54
  37.5 12.1 %all-to-all-start = ((bf16[64,8,256]{2,0,1:T(8,128)(2,1)}), bf16[64,8,256]{2,0,1:T(8,128)(2,1)S(1)}, u32[]{:S(2)}, u32[]{:S(2)}) async-start(bf16[64,8,256]{2,0,1:T(8,128)(2,1)} %bitcast.73), calls=%async_computation | async-start | bytes 524288 | tf_op jit(solution)/shard_map/all_to_all | solution.py:49
  72.0 6.0 %copy-start.1 = (bf16[8,2,128,64]{2,1,0,3:T(2,128)(2,1)S(1)}, bf16[8,2,128,64]{2,1,0,3:T(2,128)(2,1)}, u32[]{:S(2)}) copy-start(bf16[8,2,128,64]{2,1,0,3:T(2,128)(2,1)} %custom-call.6) | copy-start | bytes 786436
Sparse Core Ops, SparseCore 0:
  23.8 15.6 all-gather.2
  41.1 16.6 all-gather.4
where the time goes:
time: 150 us; the launch traced here: 149 us
  blocking collectives  42.8 us (29%)
  matrix products  39.3 us (26%)
  local copies, waits for them, and re-layouts  24.3 us (16%)
  other arithmetic  13.5 us (9%)
  between operations  13.5 us (9%)
  waiting for transfers between devices  11.2 us (7%)
  starting transfers between devices  3.63 us (2%)
    dot_general x8, matrix products, attend_block(): jnp.einsum('abd,asjd->absj', query_group, key_slots, preferred_element_ty...  22.8 us
    dot_general x8, matrix products, attend_block(): jnp.einsum('absj,asjd->abd', rounded, value_slots, preferred_element_type...  16.4 us
    all_to_all x1, blocking collectives, local(): lax.all_to_all(keys, 'uly', split_axis=1, concat_axis=0, tiled=True)  16.1 us
    all_to_all x1, blocking collectives, local(): lax.all_to_all(result, 'uly', split_axis=0, concat_axis=1, tiled=True)  14.6 us
    reshape x5, local copies, waits for them, and re-layouts, head_major(): token_rows.reshape(token_rows.shape[0] // BLOCK, BLOCK, heads_local, head...  12.4 us
    all_to_all x1, blocking collectives, local(): lax.all_to_all(values, 'uly', split_axis=1, concat_axis=0, tiled=True)  12.1 us
    all_to_all x1, waiting for transfers between devices, local(): lax.all_to_all(queries, 'uly', split_axis=1, concat_axis=0, tiled=True)  8.31 us
    gather x3, local copies, waits for them, and re-layouts, select_blocks(): return jnp.take(source, chosen, axis=0)  6.75 us
  transfers between devices with their start and end apart: 3, of which 2 were waited for; matrix products, arithmetic and copies ran while one was open for 5% of the time, Pallas kernels for 0%

commit v1 on v0

--- a/solution.py
+++ b/solution.py
@@ -1,10 +1,18 @@
+import functools
+import math
+
 import jax
 import jax.numpy as jnp
 from jax import lax
+from jax.experimental import pallas as pl
+from jax.experimental.pallas import tpu as pltpu
 from jax.sharding import PartitionSpec as P
 
 BLOCK = 128
 QGROUP = 2
+LANES = 128
+NEG = -1e30
+EVERY = ("blk", "uly")
 
 
 def head_major(token_rows, heads_local, head_dim):
@@ -39,7 +47,7 @@
     return (summed / denominator[:, :, None]).astype(jnp.bfloat16)
 
 
-def local(queries, keys, values, block_list):
+def by_context(queries, keys, values, block_list):
     heads_local = block_list.shape[0]
     blocks_dev = block_list.shape[1]
     slot_count = block_list.shape[2]
@@ -55,7 +63,6 @@
     chosen = jnp.maximum(block_list, 0)
     key_slots = jax.vmap(select_blocks)(head_major(keys_all, heads_local, head_dim), chosen)
     value_slots = jax.vmap(select_blocks)(head_major(values_all, heads_local, head_dim), chosen)
-    key_slots, value_slots = (key_slots, value_slots)
     groups = heads_local * blocks_dev // QGROUP
     query_heads = head_major(query_rows, heads_local, head_dim).reshape(
         groups, QGROUP, BLOCK, head_dim
@@ -75,6 +82,184 @@
     return lax.all_to_all(result, "uly", split_axis=0, concat_axis=1, tiled=True)
 
 
+def lane_of(shape):
+    return lax.broadcasted_iota(jnp.int32, shape, len(shape) - 1)
+
+
+def pack_kernel(nu, nb, q_ref, k_ref, v_ref, list_ref, out_ref, *rest):
+    bias_refs, bias = rest[:nb], rest[nb]
+    rows = q_ref.shape[0]
+    half, hd = rows // 2, LANES // 2
+    low = lane_of((rows, LANES)) < hd
+    low_half = lane_of((half, LANES)) < hd
+    for pair in range(q_ref.shape[1] // LANES):
+        cols = slice(pair * LANES, (pair + 1) * LANES)
+        q, k, v = q_ref[:, cols], k_ref[:, cols], v_ref[:, cols]
+        k_turned, v_turned = pltpu.roll(k, hd, 1), pltpu.roll(v, hd, 1)
+        q_turned = pltpu.roll(q, hd, 1)
+        for odd in range(2):
+            head = 2 * pair + odd
+            dest = (head % nb) * nu + head // nb
+            if odd:
+                kv = jnp.where(low, k_turned, v)
+                qq = jnp.where(low_half, q_turned[:half], q[half:])
+            else:
+                kv = jnp.where(low, k, v_turned)
+                qq = jnp.where(low_half, q[:half], q_turned[half:])
+            out_ref[dest, :rows, :] = kv
+            out_ref[dest, rows:, :] = qq
+    listed = list_ref[...]
+    lane = lane_of((listed.shape[0], LANES)) - hd
+    allowed = jnp.zeros((listed.shape[0], LANES), jnp.bool_)
+    for slot in range(listed.shape[1]):
+        allowed = allowed | (listed[:, slot : slot + 1] == lane)
+    blocks = listed.shape[0] // nb
+    all_bias = jnp.where(allowed, 0.0, NEG)
+    for head in range(nb):
+        bias[head] = all_bias[head * blocks : (head + 1) * blocks]
+    me = lax.axis_index("blk")
+    for step in range(nb):
+        bias_refs[step][...] = bias[lax.rem(me + step, nb)]
+
+
+def attend_kernel(nb, scale, g_ref, *rest):
+    bias_refs, (out_ref, qx, kx, vx, bias) = rest[:nb], rest[nb:]
+    chunks, packed, _ = g_ref.shape
+    rows = packed * 2 // 3
+    half, hd = rows // 2, LANES // 2
+    blocks = chunks * rows // BLOCK
+    here = blocks // nb
+    me = lax.axis_index("blk")
+    for step in range(nb):
+        bias[lax.rem(me + nb - step, nb)] = bias_refs[step][...]
+    lane = lane_of((rows, LANES))
+    low = lane < hd
+    low_half = lane_of((half, LANES)) < hd
+    one = jnp.ones((rows, LANES), jnp.bfloat16)
+    for t in range(chunks):
+        b = t * rows // BLOCK
+        kv = g_ref[t, :rows, :]
+        q = g_ref[t, rows:, :]
+        row = jnp.broadcast_to(bias[b // here, b % here : b % here + 1, :], (half, LANES))
+        row = row.astype(jnp.bfloat16)
+        at = t * rows
+        kx[at : at + rows, :] = jnp.where(low, kv, (lane == hd + b).astype(jnp.bfloat16))
+        vx[at : at + rows, :] = jnp.where(low, one, kv)
+        qx[at : at + half, :] = jnp.where(low_half, q, row)
+        qx[at + half : at + rows, :] = jnp.where(low_half, pltpu.roll(q, hd, 1), row)
+    group = QGROUP * BLOCK
+    later = lax.broadcasted_iota(jnp.int32, (group, group), 1) > lax.broadcasted_iota(
+        jnp.int32, (group, group), 0
+    )
+    factor = scale * math.log2(math.e)
+    for g in range(blocks // QGROUP):
+        at = g * group
+        query = qx[at : at + group, :]
+        scores = []
+        for c in range(g + 1):
+            s = lax.dot_general(
+                query,
+                kx[c * group : (c + 1) * group, :],
+                (((1,), (1,)), ((), ())),
+                preferred_element_type=jnp.float32,
+            )
+            scores.append(jnp.where(later, NEG, s) if c == g else s)
+        top = functools.reduce(jnp.maximum, scores)
+        top = jnp.max(top, axis=1, keepdims=True)
+        total = jnp.zeros((group, LANES), jnp.float32)
+        for c in range(g + 1):
+            weight = jnp.exp2((scores[c] - top) * factor).astype(jnp.bfloat16)
+            total += jnp.dot(
+                weight, vx[c * group : (c + 1) * group, :], preferred_element_type=jnp.float32
+            )
+        turned = pltpu.roll(total, hd, 1)
+        for i in range(group // rows):
+            a, m, e = i * rows, i * rows + half, (i + 1) * rows
+            upper = jnp.where(low_half, turned[a:m], total[m:e])
+            lower = jnp.where(low_half, total[a:m], turned[m:e])
+            out_ref[at // rows + i] = (upper / lower).astype(jnp.bfloat16)
+
+
+def unpack_kernel(nu, nb, g_ref, out_ref):
+    half, hd = g_ref.shape[1], LANES // 2
+    low = lane_of((half, LANES)) < hd
+    for pair in range(out_ref.shape[1] // LANES):
+        cols = slice(pair * LANES, (pair + 1) * LANES)
+        even, odd = 2 * pair, 2 * pair + 1
+        a = g_ref[(even % nb) * nu + even // nb]
+        b = g_ref[(odd % nb) * nu + odd // nb]
+        out_ref[:half, cols] = jnp.where(low, a, pltpu.roll(b, hd, 1))
+        out_ref[half:, cols] = jnp.where(low, pltpu.roll(a, hd, 1), b)
+
+
+def by_head(queries, keys, values, block_list):
+    nu, nb = lax.axis_size("uly"), lax.axis_size("blk")
+    count = nu * nb
+    rows, width = queries.shape
+    heads_local, here, slots = block_list.shape
+    head_dim = width // (heads_local * nu)
+    blocks = here * nb
+    vmem = pl.BlockSpec(memory_space=pltpu.VMEM)
+    small = jax.ShapeDtypeStruct((here, LANES), jnp.float32)
+    packed, *bias = pl.pallas_call(
+        functools.partial(pack_kernel, nu, nb),
+        out_shape=(jax.ShapeDtypeStruct((count, rows * 3 // 2, LANES), jnp.bfloat16),)
+        + (small,) * nb,
+        in_specs=[vmem] * 4,
+        out_specs=(vmem,) * (nb + 1),
+        scratch_shapes=[pltpu.VMEM((nb, here, LANES), jnp.float32)],
+        cost_estimate=pl.CostEstimate(
+            flops=4 * rows * width, bytes_accessed=12 * rows * width, transcendentals=0
+        ),
+    )(queries, keys, values, block_list.reshape(heads_local * here, slots))
+    whole = lax.all_to_all(packed, EVERY, split_axis=0, concat_axis=0)
+    moved = [bias[0]] + [
+        lax.ppermute(bias[step], "blk", [(i, (i + step) % nb) for i in range(nb)])
+        for step in range(1, nb)
+    ]
+    tokens = count * rows
+    attended = pl.pallas_call(
+        functools.partial(attend_kernel, nb, head_dim**-0.5),
+        out_shape=jax.ShapeDtypeStruct((count, rows // 2, LANES), jnp.bfloat16),
+        in_specs=[vmem] * (nb + 1),
+        out_specs=vmem,
+        scratch_shapes=[pltpu.VMEM((tokens, LANES), jnp.bfloat16)] * 3
+        + [pltpu.VMEM((nb, here, LANES), jnp.float32)],
+        cost_estimate=pl.CostEstimate(
+            flops=4 * tokens * tokens // 2 * LANES,
+            bytes_accessed=4 * tokens * LANES * 2,
+            transcendentals=tokens * tokens // 2,
+        ),
+    )(whole, *moved)
+    back = lax.all_to_all(attended, EVERY, split_axis=0, concat_axis=0)
+    return pl.pallas_call(
+        functools.partial(unpack_kernel, nu, nb),
+        out_shape=jax.ShapeDtypeStruct((rows, width), jnp.bfloat16),
+        in_specs=[vmem],
+        out_specs=vmem,
+        cost_estimate=pl.CostEstimate(
+            flops=2 * rows * width, bytes_accessed=4 * rows * width, transcendentals=0
+        ),
+    )(back)
+
+
+def local(queries, keys, values, block_list):
+    nu, nb = lax.axis_size("uly"), lax.axis_size("blk")
+    rows, width = queries.shape
+    heads_local, here, _ = block_list.shape
+    head_dim = width // (heads_local * nu)
+    blocks = here * nb
+    one_head = (
+        heads_local == nb
+        and 2 * head_dim == LANES
+        and blocks <= LANES // 2
+        and blocks % QGROUP == 0
+        and BLOCK % rows == 0
+        and rows % 32 == 0
+    )
+    return (by_head if one_head else by_context)(queries, keys, values, block_list)
+
+
 def solution(mesh):
     placed = (
         P(("blk", "uly"), None),

time: 150 us -> 54.6 us (0.36)
  matrix products: 39.3 us -> 0 us
  blocking collectives: 42.8 us -> 13.7 us
  local copies, waits for them, and re-layouts: 24.3 us -> 1.23 us
  other arithmetic: 13.5 us -> 0 us
  between operations: 13.5 us -> 0.05 us
  Pallas kernels: 0 us -> 10.5 us
  waiting for transfers between devices: 11.2 us -> 18.5 us
  starting transfers between devices: 3.63 us -> 10.3 us
    dot_general x16 -> x0, matrix products: 39.3 us -> none  [the longest x8 22.8 us: attend_block(): jnp.einsum('abd,asjd->absj', query_group, key_slots, preferred_element_ty...]
    all_to_all x3 -> x1, blocking collectives: 42.8 us -> 13.7 us  [by_head(): back = lax.all_to_all(attended, EVERY, split_axis=0, concat_axis=0)]
    reshape x6 -> x0, local copies, waits for them, and re-layouts: 12.5 us -> none  [the longest x5 12.4 us: head_major(): token_rows.reshape(token_rows.shape[0] // BLOCK, BLOCK, heads_local, head...]
    pallas_call x0 -> x3, Pallas kernels: none -> 10.5 us  [the longest x1 6.42 us: by_head(): pl.pallas_call(functools.partial(attend_kernel, nb, head_dim ** (-0.5)),...]
    all_to_all x1, waiting for transfers between devices: 8.31 us -> 16.1 us  [by_head(): whole = lax.all_to_all(packed, EVERY, split_axis=0, concat_axis=0)]
    gather x3 -> x0, local copies, waits for them, and re-layouts: 6.75 us -> none  [select_blocks(): return jnp.take(source, chosen, axis=0)]
    reduce_sum x8 -> x0, other arithmetic: 6.27 us -> none  [attend_block(): denominator = jnp.sum(weights, axis=(2, 3))]
    select_n x1 -> x0, other arithmetic: 5.95 us -> none  [select_blocks(): return jnp.take(source, chosen, axis=0)]
  transfers between devices with their start and end apart: 3 -> 4, of which waited for: 2 -> 3; matrix products, arithmetic and copies ran while one was open for 5% -> 0% of each run, Pallas kernels for 0% -> 0%
where the time goes in v1:
time: 54.6 us; the launch traced here: 54.3 us
  waiting for transfers between devices  18.5 us (34%)
  blocking collectives  13.7 us (25%)
  Pallas kernels  10.5 us (19%)
  starting transfers between devices  10.3 us (19%)
  local copies, waits for them, and re-layouts  1.23 us (2%)
    all_to_all x1, waiting for transfers between devices, by_head(): whole = lax.all_to_all(packed, EVERY, split_axis=0, concat_axis=0)  16.1 us
    all_to_all x1, blocking collectives, by_head(): back = lax.all_to_all(attended, EVERY, split_axis=0, concat_axis=0)  13.7 us
    all_to_all x1, starting transfers between devices, by_head(): whole = lax.all_to_all(packed, EVERY, split_axis=0, concat_axis=0)  7.33 us
    pallas_call x1, Pallas kernels, by_head(): pl.pallas_call(functools.partial(attend_kernel, nb, head_dim ** (-0.5)),...  6.42 us
    ppermute x3, starting transfers between devices, by_head(): lax.ppermute(bias[step], 'blk', [(i, (i + step) % nb) for i in range(nb)])  2.95 us
    ppermute x3, waiting for transfers between devices, by_head(): lax.ppermute(bias[step], 'blk', [(i, (i + step) % nb) for i in range(nb)])  2.4 us
    pallas_call x1, Pallas kernels, by_head(): pl.pallas_call(functools.partial(pack_kernel, nu, nb), out_shape=(jax.Sha...  2.27 us
    pallas_call x1, Pallas kernels, by_head(): pl.pallas_call(functools.partial(unpack_kernel, nu, nb), out_shape=jax.Sh...  1.79 us
  transfers between devices with their start and end apart: 4, of which 3 were waited for; matrix products, arithmetic and copies ran while one was open for 0% of the time, Pallas kernels for 0%

profile of v1, /device:TPU:0, one launch (start us, length us, event | category | flops | bytes accessed | tf_op | source)
XLA Modules:
  0.0 54.3 jit_solution(8635562253267484183)
XLA Ops:
  0.0 2.3 %shard_map.46 = (bf16[32,96,128]{2,1,0:T(8,128)(2,1)}, f32[4,128]{1,0:T(4,128)}, f32[4,128]{1,0:T(4,128)}, f32[4,128]{1,0:T(4,128)}, f32[4,128]{1,0:T(4,128)}) custom-call(bf16[64,2048]{1,0:T(8,128)(2,1)} %q_ref.1, bf16[64,2048]{1,0:T(8,128)(2,1)} %k_ref.1, bf16[64,2048]{1,0:T(8,128)(2,1)} %v_ref.1, s32[16,16]{1,0:T(8,128)} %bitcast.1), custom_call_target="tpu_custom_call" | custom-call | flops 524288 | bytes 1572864 | tf_op jit(solution)/shard_map/pallas_call | solution.py:204
  2.3 0.0 copy-start.6
  2.3 7.3 %all-to-all-start = ((bf16[32,96,128]{2,1,0:T(8,128)(2,1)}), bf16[32,96,128]{2,1,0:T(8,128)(2,1)S(1)}, u32[]{:S(2)}, u32[]{:S(2)}) async-start(bf16[32,96,128]{2,1,0:T(8,128)(2,1)} %get-tuple-element.10), calls=%async_computation | async-start | bytes 1572864 | tf_op jit(solution)/shard_map/all_to_all | solution.py:215
  9.6 0.0 copy-start.4
  9.6 0.0 copy-done.6
  9.6 0.0 copy-start.2
  9.6 0.3 collective-permute-start
  9.9 0.3 copy-done.4
  10.3 1.8 %collective-permute-start.1 = (f32[4,128]{1,0:T(4,128)S(1)}, f32[4,128]{1,0:T(4,128)S(1)}, u32[]{:S(2)}, u32[]{:S(2)}) collective-permute-start(f32[4,128]{1,0:T(4,128)S(1)} %copy-done.4), channel_id=1, source_target_pairs={{0,2},{1,3},{2,0},{3,1},{4,6},{5,7},{6,4},{7,5},{8,10},{9,11},{10,... | collective-permute-start | bytes 6152 | tf_op jit(solution)/shard_map/ppermute | solution.py:217
  12.0 0.0 copy-done.2
  12.0 0.9 %collective-permute-start.2 = (f32[4,128]{1,0:T(4,128)S(1)}, f32[4,128]{1,0:T(4,128)S(1)}, u32[]{:S(2)}, u32[]{:S(2)}) collective-permute-start(f32[4,128]{1,0:T(4,128)S(1)} %copy-done.2), channel_id=1, source_target_pairs={{0,3},{1,0},{2,1},{3,2},{4,7},{5,4},{6,5},{7,6},{8,11},{9,8},{10,9... | collective-permute-start | bytes 6152 | tf_op jit(solution)/shard_map/ppermute | solution.py:217
  12.9 1.6 %collective-permute-done.rest_1_ = f32[4,128]{1,0:T(4,128)S(1)} collective-permute-done((f32[4,128]{1,0:T(4,128)S(1)}, f32[4,128]{1,0:T(4,128)S(1)}, u32[]{:S(2)}, u32[]{:S(2)}) %collective-permute-start) | collective-permute-done | bytes 2080 | tf_op jit(solution)/shard_map/ppermute | solution.py:217
  14.5 0.0 copy-start.1
  14.5 0.8 %collective-permute-done.1.rest_2_ = f32[4,128]{1,0:T(4,128)S(1)} collective-permute-done((f32[4,128]{1,0:T(4,128)S(1)}, f32[4,128]{1,0:T(4,128)S(1)}, u32[]{:S(2)}, u32[]{:S(2)}) %collective-permute-start.1) | collective-permute-done | bytes 2080 | tf_op jit(solution)/shard_map/ppermute | solution.py:217
  15.3 0.0 copy-start.3
  15.3 0.0 collective-permute-done.2.rest_3_
  15.3 0.0 copy-start.5
  15.3 16.1 %all-to-all-done.g_ref = bf16[32,96,128]{2,1,0:T(8,128)(2,1)S(1)} async-done(((bf16[32,96,128]{2,1,0:T(8,128)(2,1)}), bf16[32,96,128]{2,1,0:T(8,128)(2,1)S(1)}, u32[]{:S(2)}, u32[]{:S(2)}) %all-to-all-start) | async-done | bytes 786464 | tf_op jit(solution)/shard_map/all_to_all | solution.py:215
  31.5 0.0 copy-start
  31.5 0.0 copy-done.1
  31.5 0.0 copy-done.3
  31.5 0.0 copy-done.5
  31.5 0.9 %copy-done = bf16[32,96,128]{2,1,0:T(8,128)(2,1)} copy-done((bf16[32,96,128]{2,1,0:T(8,128)(2,1)}, bf16[32,96,128]{2,1,0:T(8,128)(2,1)S(1)}, u32[]{:S(2)}) %copy-start) | copy-done | bytes 786456
  32.3 6.4 %shard_map.47 = bf16[32,32,128]{2,1,0:T(8,128)(2,1)} custom-call(bf16[32,96,128]{2,1,0:T(8,128)(2,1)} %copy-done, f32[4,128]{1,0:T(4,128)} %get-tuple-element.11.rest_0_, f32[4,128]{1,0:T(4,128)} %copy-done.1, f32[4,128]{1,0:T(4,128)} %copy-done.3, f32[4,128]{1,0:T(4,128)} %copy-done.5), custom_call_target="tpu_custom_call" | custom-call | flops 1073741824 | bytes 2097152 | tf_op jit(solution)/shard_map/pallas_call | solution.py:221
  38.8 13.7 %all_to_all.10.g_ref = bf16[32,32,128]{2,1,0:T(8,128)(2,1)} all-to-all(bf16[32,32,128]{2,1,0:T(8,128)(2,1)} %shard_map.47), channel_id=1, replica_groups=mesh['uly'=8,'blk'=4] {'blk','uly'}, dimensions={0} | all-to-all | bytes 524288 | tf_op jit(solution)/shard_map/all_to_all | solution.py:234
  52.5 1.8 %shard_map.48 = bf16[64,2048]{1,0:T(8,128)(2,1)} custom-call(bf16[32,32,128]{2,1,0:T(8,128)(2,1)} %all_to_all.10.g_ref), custom_call_target="tpu_custom_call" | custom-call | flops 262144 | bytes 524288 | tf_op jit(solution)/shard_map/pallas_call | solution.py:235
Async XLA Ops:
  2.3 7.3 %copy-start.6 = (f32[4,128]{1,0:T(4,128)S(1)}, f32[4,128]{1,0:T(4,128)}, u32[]{:S(2)}) copy-start(f32[4,128]{1,0:T(4,128)} %get-tuple-element.12) | copy-start | bytes 6148
  2.3 29.2 %all-to-all-start = ((bf16[32,96,128]{2,1,0:T(8,128)(2,1)}), bf16[32,96,128]{2,1,0:T(8,128)(2,1)S(1)}, u32[]{:S(2)}, u32[]{:S(2)}) async-start(bf16[32,96,128]{2,1,0:T(8,128)(2,1)} %get-tuple-element.10), calls=%async_computation | async-start | bytes 1572864 | tf_op jit(solution)/shard_map/all_to_all | solution.py:215
  9.6 0.7 %copy-start.4 = (f32[4,128]{1,0:T(4,128)S(1)}, f32[4,128]{1,0:T(4,128)}, u32[]{:S(2)}) copy-start(f32[4,128]{1,0:T(4,128)} %get-tuple-element.13) | copy-start | bytes 6148
  9.6 2.4 %copy-start.2 = (f32[4,128]{1,0:T(4,128)S(1)}, f32[4,128]{1,0:T(4,128)}, u32[]{:S(2)}) copy-start(f32[4,128]{1,0:T(4,128)} %get-tuple-element.14) | copy-start | bytes 6148
  9.6 4.9 %collective-permute-start = (f32[4,128]{1,0:T(4,128)S(1)}, f32[4,128]{1,0:T(4,128)S(1)}, u32[]{:S(2)}, u32[]{:S(2)}) collective-permute-start(f32[4,128]{1,0:T(4,128)S(1)} %copy-done.6), channel_id=1, source_target_pairs={{0,1},{1,2},{2,3},{3,0},{4,5},{5,6},{6,7},{7,4},{8,9},{9,10},{10,1... | collective-permute-start | bytes 6152 | tf_op jit(solution)/shard_map/ppermute | solution.py:217
  10.3 5.0 %collective-permute-start.1 = (f32[4,128]{1,0:T(4,128)S(1)}, f32[4,128]{1,0:T(4,128)S(1)}, u32[]{:S(2)}, u32[]{:S(2)}) collective-permute-start(f32[4,128]{1,0:T(4,128)S(1)} %copy-done.4), channel_id=1, source_target_pairs={{0,2},{1,3},{2,0},{3,1},{4,6},{5,7},{6,4},{7,5},{8,10},{9,11},{10,... | collective-permute-start | bytes 6152 | tf_op jit(solution)/shard_map/ppermute | solution.py:217
  12.0 3.3 %collective-permute-start.2 = (f32[4,128]{1,0:T(4,128)S(1)}, f32[4,128]{1,0:T(4,128)S(1)}, u32[]{:S(2)}, u32[]{:S(2)}) collective-permute-start(f32[4,128]{1,0:T(4,128)S(1)} %copy-done.2), channel_id=1, source_target_pairs={{0,3},{1,0},{2,1},{3,2},{4,7},{5,4},{6,5},{7,6},{8,11},{9,8},{10,9... | collective-permute-start | bytes 6152 | tf_op jit(solution)/shard_map/ppermute | solution.py:217
  14.5 16.9 %copy-start.1 = (f32[4,128]{1,0:T(4,128)}, f32[4,128]{1,0:T(4,128)S(1)}, u32[]{:S(2)}) copy-start(f32[4,128]{1,0:T(4,128)S(1)} %collective-permute-done.rest_1_) | copy-start | bytes 6148
  15.3 16.1 %copy-start.3 = (f32[4,128]{1,0:T(4,128)}, f32[4,128]{1,0:T(4,128)S(1)}, u32[]{:S(2)}) copy-start(f32[4,128]{1,0:T(4,128)S(1)} %collective-permute-done.1.rest_2_) | copy-start | bytes 6148
  15.3 16.1 %copy-start.5 = (f32[4,128]{1,0:T(4,128)}, f32[4,128]{1,0:T(4,128)S(1)}, u32[]{:S(2)}) copy-start(f32[4,128]{1,0:T(4,128)S(1)} %collective-permute-done.2.rest_3_) | copy-start | bytes 6148
  31.5 0.9 %copy-start = (bf16[32,96,128]{2,1,0:T(8,128)(2,1)}, bf16[32,96,128]{2,1,0:T(8,128)(2,1)S(1)}, u32[]{:S(2)}) copy-start(bf16[32,96,128]{2,1,0:T(8,128)(2,1)S(1)} %all-to-all-done.g_ref) | copy-start | bytes 2359300

commit v2 on v1

--- a/solution.py
+++ b/solution.py
@@ -192,6 +192,10 @@
         out_ref[half:, cols] = jnp.where(low, pltpu.roll(a, hd, 1), b)
 
 
+def in_vmem(x):
+    return pltpu.with_memory_space_constraint(x, pltpu.VMEM)
+
+
 def by_head(queries, keys, values, block_list):
     nu, nb = lax.axis_size("uly"), lax.axis_size("blk")
     count = nu * nb
@@ -200,11 +204,10 @@
     head_dim = width // (heads_local * nu)
     blocks = here * nb
     vmem = pl.BlockSpec(memory_space=pltpu.VMEM)
-    small = jax.ShapeDtypeStruct((here, LANES), jnp.float32)
+    small = pltpu.VMEM((here, LANES), jnp.float32)
     packed, *bias = pl.pallas_call(
         functools.partial(pack_kernel, nu, nb),
-        out_shape=(jax.ShapeDtypeStruct((count, rows * 3 // 2, LANES), jnp.bfloat16),)
-        + (small,) * nb,
+        out_shape=(pltpu.VMEM((count, rows * 3 // 2, LANES), jnp.bfloat16),) + (small,) * nb,
         in_specs=[vmem] * 4,
         out_specs=(vmem,) * (nb + 1),
         scratch_shapes=[pltpu.VMEM((nb, here, LANES), jnp.float32)],
@@ -220,7 +223,7 @@
     tokens = count * rows
     attended = pl.pallas_call(
         functools.partial(attend_kernel, nb, head_dim**-0.5),
-        out_shape=jax.ShapeDtypeStruct((count, rows // 2, LANES), jnp.bfloat16),
+        out_shape=pltpu.VMEM((count, rows // 2, LANES), jnp.bfloat16),
         in_specs=[vmem] * (nb + 1),
         out_specs=vmem,
         scratch_shapes=[pltpu.VMEM((tokens, LANES), jnp.bfloat16)] * 3
@@ -230,7 +233,7 @@
             bytes_accessed=4 * tokens * LANES * 2,
             transcendentals=tokens * tokens // 2,
         ),
-    )(whole, *moved)
+    )(*(in_vmem(x) for x in (whole, *moved)))
     back = lax.all_to_all(attended, EVERY, split_axis=0, concat_axis=0)
     return pl.pallas_call(
         functools.partial(unpack_kernel, nu, nb),
@@ -240,7 +243,7 @@
         cost_estimate=pl.CostEstimate(
             flops=2 * rows * width, bytes_accessed=4 * rows * width, transcendentals=0
         ),
-    )(back)
+    )(in_vmem(back))
 
 
 def local(queries, keys, values, block_list):

time: 54.6 us -> 49.7 us (0.910)
  Pallas kernels: 10.5 us -> 7.66 us
  local copies, waits for them, and re-layouts: 1.23 us -> 0 us
  blocking collectives: 13.7 us -> 12.6 us
    pallas_call x1, Pallas kernels: 6.42 us -> 4.54 us  [by_head(): pl.pallas_call(functools.partial(attend_kernel, nb, head_dim ** (-0.5)),...]
    unnamed x14 -> x0, local copies, waits for them, and re-layouts: 1.23 us -> none
    all_to_all x1, blocking collectives: 13.7 us -> 12.6 us  [by_head(): back = lax.all_to_all(attended, EVERY, split_axis=0, concat_axis=0)]
    pallas_call x1, Pallas kernels: 1.79 us -> 0.84 us  [by_head(): pl.pallas_call(functools.partial(unpack_kernel, nu, nb), out_shape=jax.Sh...]
where the time goes in v2:
time: 49.7 us; the launch traced here: 49.5 us
  waiting for transfers between devices  18.6 us (37%)
  blocking collectives  12.6 us (25%)
  starting transfers between devices  10.6 us (21%)
  Pallas kernels  7.66 us (15%)
    all_to_all x1, waiting for transfers between devices, by_head(): whole = lax.all_to_all(packed, EVERY, split_axis=0, concat_axis=0)  16.1 us
    all_to_all x1, blocking collectives, by_head(): back = lax.all_to_all(attended, EVERY, split_axis=0, concat_axis=0)  12.6 us
    all_to_all x1, starting transfers between devices, by_head(): whole = lax.all_to_all(packed, EVERY, split_axis=0, concat_axis=0)  7.33 us
    pallas_call x1, Pallas kernels, by_head(): pl.pallas_call(functools.partial(attend_kernel, nb, head_dim ** (-0.5)),...  4.54 us
    ppermute x3, starting transfers between devices, by_head(): lax.ppermute(bias[step], 'blk', [(i, (i + step) % nb) for i in range(nb)])  3.28 us
    ppermute x3, waiting for transfers between devices, by_head(): lax.ppermute(bias[step], 'blk', [(i, (i + step) % nb) for i in range(nb)])  2.43 us
    pallas_call x1, Pallas kernels, by_head(): pl.pallas_call(functools.partial(pack_kernel, nu, nb), out_shape=(pltpu.V...  2.28 us
  transfers between devices with their start and end apart: 4, of which 3 were waited for; matrix products, arithmetic and copies ran while one was open for 0% of the time, Pallas kernels for 0%

profile of v2, /device:TPU:0, one launch (start us, length us, event | category | flops | bytes accessed | tf_op | source)
XLA Modules:
  0.0 49.5 jit_solution(13134494770292322706)
XLA Ops:
  0.0 2.3 %shard_map.46 = (bf16[32,96,128]{2,1,0:T(8,128)(2,1)}, f32[4,128]{1,0:T(4,128)S(1)}, f32[4,128]{1,0:T(4,128)S(1)}, f32[4,128]{1,0:T(4,128)S(1)}, f32[4,128]{1,0:T(4,128)S(1)}) custom-call(bf16[64,2048]{1,0:T(8,128)(2,1)} %q_ref.1, bf16[64,2048]{1,0:T(8,128)(2,1)} %k_ref.1, bf16[64,2048]{1,0:T(8,128)(2,1)} %v_ref.1, s32[16,16]{1,0:T(8,128)} %bitcast.1), custom_call_target="tpu_custom_call" | custom-call | flops 524288 | bytes 1572864 | tf_op jit(solution)/shard_map/pallas_call | solution.py:208
  2.3 7.3 %all-to-all-start = ((bf16[32,96,128]{2,1,0:T(8,128)(2,1)}), bf16[32,96,128]{2,1,0:T(8,128)(2,1)S(1)}, u32[]{:S(2)}, u32[]{:S(2)}) async-start(bf16[32,96,128]{2,1,0:T(8,128)(2,1)} %get-tuple-element.10), calls=%async_computation | async-start | bytes 1572864 | tf_op jit(solution)/shard_map/all_to_all | solution.py:218
  9.6 0.3 collective-permute-start
  9.9 1.6 %collective-permute-start.1 = (f32[4,128]{1,0:T(4,128)S(1)}, f32[4,128]{1,0:T(4,128)S(1)}, u32[]{:S(2)}, u32[]{:S(2)}) collective-permute-start(f32[4,128]{1,0:T(4,128)S(1)} %get-tuple-element.13), channel_id=1, source_target_pairs={{0,2},{1,3},{2,0},{3,1},{4,6},{5,7},{6,4},{7,5},{8,10},{9,11},{10,... | collective-permute-start | bytes 6152 | tf_op jit(solution)/shard_map/ppermute | solution.py:220
  11.5 1.4 %collective-permute-start.2 = (f32[4,128]{1,0:T(4,128)S(1)}, f32[4,128]{1,0:T(4,128)S(1)}, u32[]{:S(2)}, u32[]{:S(2)}) collective-permute-start(f32[4,128]{1,0:T(4,128)S(1)} %get-tuple-element.14), channel_id=1, source_target_pairs={{0,3},{1,0},{2,1},{3,2},{4,7},{5,4},{6,5},{7,6},{8,11},{9,8},{10,9... | collective-permute-start | bytes 6152 | tf_op jit(solution)/shard_map/ppermute | solution.py:220
  12.9 1.6 %collective-permute-done.rest_1_ = f32[4,128]{1,0:T(4,128)S(1)} collective-permute-done((f32[4,128]{1,0:T(4,128)S(1)}, f32[4,128]{1,0:T(4,128)S(1)}, u32[]{:S(2)}, u32[]{:S(2)}) %collective-permute-start) | collective-permute-done | bytes 2080 | tf_op jit(solution)/shard_map/ppermute | solution.py:220
  14.5 0.8 %collective-permute-done.1.rest_2_ = f32[4,128]{1,0:T(4,128)S(1)} collective-permute-done((f32[4,128]{1,0:T(4,128)S(1)}, f32[4,128]{1,0:T(4,128)S(1)}, u32[]{:S(2)}, u32[]{:S(2)}) %collective-permute-start.1) | collective-permute-done | bytes 2080 | tf_op jit(solution)/shard_map/ppermute | solution.py:220
  15.3 0.0 collective-permute-done.2.rest_3_
  15.3 16.1 %all-to-all-done.g_ref = bf16[32,96,128]{2,1,0:T(8,128)(2,1)S(1)} async-done(((bf16[32,96,128]{2,1,0:T(8,128)(2,1)}), bf16[32,96,128]{2,1,0:T(8,128)(2,1)S(1)}, u32[]{:S(2)}, u32[]{:S(2)}) %all-to-all-start) | async-done | bytes 786464 | tf_op jit(solution)/shard_map/all_to_all | solution.py:218
  31.5 4.5 %shard_map.47 = bf16[32,32,128]{2,1,0:T(8,128)(2,1)S(1)} custom-call(bf16[32,96,128]{2,1,0:T(8,128)(2,1)S(1)} %all-to-all-done.g_ref, f32[4,128]{1,0:T(4,128)S(1)} %get-tuple-element.11.rest_0_, f32[4,128]{1,0:T(4,128)S(1)} %collective-permute-done.rest_1_, f32[4,128]{1,0:T(4,128)S(1)} %collective-permute-done.1.rest_2_, ...), custom_call_target="tpu_custom_call" | custom-call | flops 1073741824 | bytes 2097152 | tf_op jit(solution)/shard_map/pallas_call | solution.py:224
  36.0 12.6 %all_to_all.10.g_ref = bf16[32,32,128]{2,1,0:T(8,128)(2,1)S(1)} all-to-all(bf16[32,32,128]{2,1,0:T(8,128)(2,1)S(1)} %shard_map.47), channel_id=1, replica_groups=mesh['uly'=8,'blk'=4] {'blk','uly'}, dimensions={0} | all-to-all | bytes 524288 | tf_op jit(solution)/shard_map/all_to_all | solution.py:237
  48.6 0.8 %shard_map.48 = bf16[64,2048]{1,0:T(8,128)(2,1)} custom-call(bf16[32,32,128]{2,1,0:T(8,128)(2,1)S(1)} %all_to_all.10.g_ref), custom_call_target="tpu_custom_call" | custom-call | flops 262144 | bytes 524288 | tf_op jit(solution)/shard_map/pallas_call | solution.py:238
Async XLA Ops:
  2.3 29.2 %all-to-all-start = ((bf16[32,96,128]{2,1,0:T(8,128)(2,1)}), bf16[32,96,128]{2,1,0:T(8,128)(2,1)S(1)}, u32[]{:S(2)}, u32[]{:S(2)}) async-start(bf16[32,96,128]{2,1,0:T(8,128)(2,1)} %get-tuple-element.10), calls=%async_computation | async-start | bytes 1572864 | tf_op jit(solution)/shard_map/all_to_all | solution.py:218
  9.6 4.9 %collective-permute-start = (f32[4,128]{1,0:T(4,128)S(1)}, f32[4,128]{1,0:T(4,128)S(1)}, u32[]{:S(2)}, u32[]{:S(2)}) collective-permute-start(f32[4,128]{1,0:T(4,128)S(1)} %get-tuple-element.12), channel_id=1, source_target_pairs={{0,1},{1,2},{2,3},{3,0},{4,5},{5,6},{6,7},{7,4},{8,9},{9,10},{10,1... | collective-permute-start | bytes 6152 | tf_op jit(solution)/shard_map/ppermute | solution.py:220
  9.9 5.4 %collective-permute-start.1 = (f32[4,128]{1,0:T(4,128)S(1)}, f32[4,128]{1,0:T(4,128)S(1)}, u32[]{:S(2)}, u32[]{:S(2)}) collective-permute-start(f32[4,128]{1,0:T(4,128)S(1)} %get-tuple-element.13), channel_id=1, source_target_pairs={{0,2},{1,3},{2,0},{3,1},{4,6},{5,7},{6,4},{7,5},{8,10},{9,11},{10,... | collective-permute-start | bytes 6152 | tf_op jit(solution)/shard_map/ppermute | solution.py:220
  11.5 3.8 %collective-permute-start.2 = (f32[4,128]{1,0:T(4,128)S(1)}, f32[4,128]{1,0:T(4,128)S(1)}, u32[]{:S(2)}, u32[]{:S(2)}) collective-permute-start(f32[4,128]{1,0:T(4,128)S(1)} %get-tuple-element.14), channel_id=1, source_target_pairs={{0,3},{1,0},{2,1},{3,2},{4,7},{5,4},{6,5},{7,6},{8,11},{9,8},{10,9... | collective-permute-start | bytes 6152 | tf_op jit(solution)/shard_map/ppermute | solution.py:220

commit v3 on v2

--- a/solution.py
+++ b/solution.py
@@ -12,6 +12,8 @@
 QGROUP = 2
 LANES = 128
 NEG = -1e30
+ONES = 16
+PIECES = 4
 EVERY = ("blk", "uly")
 
 
@@ -86,44 +88,73 @@
     return lax.broadcasted_iota(jnp.int32, shape, len(shape) - 1)
 
 
-def pack_kernel(nu, nb, q_ref, k_ref, v_ref, list_ref, out_ref, *rest):
-    bias_refs, bias = rest[:nb], rest[nb]
-    rows = q_ref.shape[0]
+def pack_kernel(
+    nu, nb, q_hbm, k_hbm, v_hbm, list_hbm, out_hbm, *rest
+):
+    bias_refs, (qkv, listed, packed, bias, in_sems, out_sems, list_sem) = rest[:nb], rest[nb:]
+    rows, width = q_hbm.shape
     half, hd = rows // 2, LANES // 2
+    pieces = in_sems.shape[0]
+    wide, owners = width // pieces, nu // pieces
     low = lane_of((rows, LANES)) < hd
     low_half = lane_of((half, LANES)) < hd
-    for pair in range(q_ref.shape[1] // LANES):
-        cols = slice(pair * LANES, (pair + 1) * LANES)
-        q, k, v = q_ref[:, cols], k_ref[:, cols], v_ref[:, cols]
-        k_turned, v_turned = pltpu.roll(k, hd, 1), pltpu.roll(v, hd, 1)
-        q_turned = pltpu.roll(q, hd, 1)
-        for odd in range(2):
-            head = 2 * pair + odd
-            dest = (head % nb) * nu + head // nb
-            if odd:
-                kv = jnp.where(low, k_turned, v)
-                qq = jnp.where(low_half, q_turned[:half], q[half:])
-            else:
-                kv = jnp.where(low, k, v_turned)
-                qq = jnp.where(low_half, q[:half], q_turned[half:])
-            out_ref[dest, :rows, :] = kv
-            out_ref[dest, rows:, :] = qq
-    listed = list_ref[...]
-    lane = lane_of((listed.shape[0], LANES)) - hd
-    allowed = jnp.zeros((listed.shape[0], LANES), jnp.bool_)
-    for slot in range(listed.shape[1]):
-        allowed = allowed | (listed[:, slot : slot + 1] == lane)
-    blocks = listed.shape[0] // nb
+    reads, writes = [], []
+    for piece in range(pieces):
+        cols = pl.ds(piece * wide, wide)
+        reads.append(
+            [
+                pltpu.make_async_copy(
+                    ref.at[:, cols], qkv.at[at, :, cols], in_sems.at[piece, at]
+                )
+                for at, ref in enumerate((q_hbm, k_hbm, v_hbm))
+            ]
+        )
+        for copy in reads[-1]:
+            copy.start()
+    list_read = pltpu.make_async_copy(list_hbm, listed, list_sem)
+    list_read.start()
+    for piece in range(pieces):
+        for copy in reads[piece]:
+            copy.wait()
+        for pair in range(piece * wide // LANES, (piece + 1) * wide // LANES):
+            cols = slice(pair * LANES, (pair + 1) * LANES)
+            q, k, v = qkv[0, :, cols], qkv[1, :, cols], qkv[2, :, cols]
+            k_turned, v_turned = pltpu.roll(k, hd, 1), pltpu.roll(v, hd, 1)
+            q_turned = pltpu.roll(q, hd, 1)
+            for odd in range(2):
+                head = 2 * pair + odd
+                if odd:
+                    kv = jnp.where(low, k_turned, v)
+                    qq = jnp.where(low_half, q_turned[:half], q[half:])
+                else:
+                    kv = jnp.where(low, k, v_turned)
+                    qq = jnp.where(low_half, q[:half], q_turned[half:])
+                packed[head % nb, head // nb, :rows, :] = kv
+                packed[head % nb, head // nb, rows:, :] = qq
+        some = pl.ds(piece * owners, owners)
+        writes.append(
+            pltpu.make_async_copy(packed.at[:, some], out_hbm.at[:, some], out_sems.at[piece])
+        )
+        writes[-1].start()
+    list_read.wait()
+    slots = listed[...]
+    lane = lane_of((slots.shape[0], LANES)) - hd
+    allowed = jnp.zeros((slots.shape[0], LANES), jnp.bool_)
+    for slot in range(slots.shape[1]):
+        allowed = allowed | (slots[:, slot : slot + 1] == lane)
+    blocks = slots.shape[0] // nb
     all_bias = jnp.where(allowed, 0.0, NEG)
     for head in range(nb):
         bias[head] = all_bias[head * blocks : (head + 1) * blocks]
     me = lax.axis_index("blk")
     for step in range(nb):
         bias_refs[step][...] = bias[lax.rem(me + step, nb)]
+    for copy in writes:
+        copy.wait()
 
 
 def attend_kernel(nb, scale, g_ref, *rest):
-    bias_refs, (out_ref, qx, kx, vx, bias) = rest[:nb], rest[nb:]
+    bias_refs, (out_ref, qx, kx, vt, st, pt, bias) = rest[:nb], rest[nb:]
     chunks, packed, _ = g_ref.shape
     rows = packed * 2 // 3
     half, hd = rows // 2, LANES // 2
@@ -135,49 +166,71 @@
     lane = lane_of((rows, LANES))
     low = lane < hd
     low_half = lane_of((half, LANES)) < hd
-    one = jnp.ones((rows, LANES), jnp.bfloat16)
-    for t in range(chunks):
-        b = t * rows // BLOCK
-        kv = g_ref[t, :rows, :]
-        q = g_ref[t, rows:, :]
-        row = jnp.broadcast_to(bias[b // here, b % here : b % here + 1, :], (half, LANES))
-        row = row.astype(jnp.bfloat16)
-        at = t * rows
-        kx[at : at + rows, :] = jnp.where(low, kv, (lane == hd + b).astype(jnp.bfloat16))
-        vx[at : at + rows, :] = jnp.where(low, one, kv)
-        qx[at : at + half, :] = jnp.where(low_half, q, row)
-        qx[at + half : at + rows, :] = jnp.where(low_half, pltpu.roll(q, hd, 1), row)
     group = QGROUP * BLOCK
-    later = lax.broadcasted_iota(jnp.int32, (group, group), 1) > lax.broadcasted_iota(
-        jnp.int32, (group, group), 0
-    )
+    each = group // rows
+    mid = group // 2
+    ones = vt.shape[0] - hd
+    vt[:ones, :] = jnp.ones((ones, vt.shape[1]), jnp.bfloat16)
+    def prepare(g):
+        for t in range(g * each, (g + 1) * each):
+            b = t * rows // BLOCK
+            kv = g_ref[t, :rows, :]
+            q = g_ref[t, rows:, :]
+            row = jnp.broadcast_to(bias[b // here, b % here : b % here + 1, :], (half, LANES))
+            row = row.astype(jnp.bfloat16)
+            kx[t * rows : (t + 1) * rows, :] = jnp.where(low, kv, (lane == hd + b).astype(jnp.bfloat16))
+            at = t // each * group + t % each * half
+            qx[at : at + half, :] = jnp.where(low_half, q, row)
+            qx[at + mid : at + mid + half, :] = jnp.where(low_half, pltpu.roll(q, hd, 1), row)
+        for b in range(g * QGROUP, (g + 1) * QGROUP):
+            pair = jnp.concatenate([g_ref[b * BLOCK // rows + i, :rows, :] for i in range(BLOCK // rows)], axis=0)
+            vt[ones:, b * BLOCK : (b + 1) * BLOCK] = pair.T[hd:, :]
+    key = lax.broadcasted_iota(jnp.int32, (group, group), 0)
+    col = lax.broadcasted_iota(jnp.int32, (group, group), 1)
+    token = col % mid // half * rows + col // mid * half + col % half
+    later = key > token
     factor = scale * math.log2(math.e)
-    for g in range(blocks // QGROUP):
-        at = g * group
-        query = qx[at : at + group, :]
-        scores = []
-        for c in range(g + 1):
-            s = lax.dot_general(
-                query,
-                kx[c * group : (c + 1) * group, :],
-                (((1,), (1,)), ((), ())),
-                preferred_element_type=jnp.float32,
-            )
-            scores.append(jnp.where(later, NEG, s) if c == g else s)
-        top = functools.reduce(jnp.maximum, scores)
-        top = jnp.max(top, axis=1, keepdims=True)
-        total = jnp.zeros((group, LANES), jnp.float32)
-        for c in range(g + 1):
-            weight = jnp.exp2((scores[c] - top) * factor).astype(jnp.bfloat16)
-            total += jnp.dot(
-                weight, vx[c * group : (c + 1) * group, :], preferred_element_type=jnp.float32
-            )
-        turned = pltpu.roll(total, hd, 1)
-        for i in range(group // rows):
-            a, m, e = i * rows, i * rows + half, (i + 1) * rows
-            upper = jnp.where(low_half, turned[a:m], total[m:e])
-            lower = jnp.where(low_half, total[a:m], turned[m:e])
-            out_ref[at // rows + i] = (upper / lower).astype(jnp.bfloat16)
+    def score(slot, g, c, top):
+        s = lax.dot_general(
+            kx[c * group : (c + 1) * group, :],
+            qx[g * group : (g + 1) * group, :],
+            (((1,), (1,)), ((), ())),
+            preferred_element_type=jnp.float32,
+        )
+        if c == g:
+            s = jnp.where(later, NEG, s)
+        st[slot, c * group : (c + 1) * group, :] = s
+        m = jnp.max(s.reshape(group // 8, 8, group), axis=0)
+        return m if top is None else jnp.maximum(top, m)
+    def weigh(slot, c, top):
+        s = st[slot, c * group : (c + 1) * group, :]
+        pt[slot, c * group : (c + 1) * group, :] = jnp.exp2((s - top) * factor).astype(jnp.bfloat16)
+    def finish(slot, g):
+        n = (g + 1) * group
+        total = jnp.dot(vt[:, :n], pt[slot, :n, :], preferred_element_type=jnp.float32)
+        result = total[ones:] / total[:1]
+        pair = jnp.concatenate([result[:, :mid], result[:, mid:]], axis=0)
+        out_ref[g * each : (g + 1) * each] = pair.T.astype(jnp.bfloat16).reshape(each, half, LANES)
+    ready = set()
+    def need(g):
+        for i in range(g + 1):
+            if i not in ready:
+                ready.add(i); prepare(i)
+    n = blocks // QGROUP
+    order = list(range(n))
+    prev = None
+    for i, g in enumerate(list(order) + [None]):
+        slot = i % 2
+        a = [] if g is None else list(range(g + 1))
+        b = [] if prev is None else list(range(prev[0] + 1))
+        if g is not None: need(g)
+        top = None
+        for j in range(max(len(a), len(b))):
+            if j < len(a): top = score(slot, g, a[j], top)
+            if j < len(b): weigh(1 - slot, b[j], prev[1])
+        if prev is not None: finish(1 - slot, prev[0])
+        if g is not None:
+            prev = (g, jnp.max(top, axis=0, keepdims=True))
 
 
 def unpack_kernel(nu, nb, g_ref, out_ref):
@@ -205,16 +258,28 @@
     blocks = here * nb
     vmem = pl.BlockSpec(memory_space=pltpu.VMEM)
     small = pltpu.VMEM((here, LANES), jnp.float32)
+    anywhere = pl.BlockSpec(memory_space=pl.ANY)
+    pieces = math.gcd(nu, PIECES)
     packed, *bias = pl.pallas_call(
         functools.partial(pack_kernel, nu, nb),
-        out_shape=(pltpu.VMEM((count, rows * 3 // 2, LANES), jnp.bfloat16),) + (small,) * nb,
-        in_specs=[vmem] * 4,
-        out_specs=(vmem,) * (nb + 1),
-        scratch_shapes=[pltpu.VMEM((nb, here, LANES), jnp.float32)],
+        out_shape=(jax.ShapeDtypeStruct((nb, nu, rows * 3 // 2, LANES), jnp.bfloat16),)
+        + (small,) * nb,
+        in_specs=[anywhere] * 4,
+        out_specs=(anywhere,) + (vmem,) * nb,
+        scratch_shapes=[
+            pltpu.VMEM((3, rows, width), jnp.bfloat16),
+            pltpu.VMEM((heads_local * here, slots), jnp.int32),
+            pltpu.VMEM((nb, nu, rows * 3 // 2, LANES), jnp.bfloat16),
+            pltpu.VMEM((nb, here, LANES), jnp.float32),
+            pltpu.SemaphoreType.DMA((pieces, 3)),
+            pltpu.SemaphoreType.DMA((pieces,)),
+            pltpu.SemaphoreType.DMA,
+        ],
         cost_estimate=pl.CostEstimate(
             flops=4 * rows * width, bytes_accessed=12 * rows * width, transcendentals=0
         ),
     )(queries, keys, values, block_list.reshape(heads_local * here, slots))
+    packed = packed.reshape(count, rows * 3 // 2, LANES)
     whole = lax.all_to_all(packed, EVERY, split_axis=0, concat_axis=0)
     moved = [bias[0]] + [
         lax.ppermute(bias[step], "blk", [(i, (i + step) % nb) for i in range(nb)])
@@ -226,8 +291,14 @@
         out_shape=pltpu.VMEM((count, rows // 2, LANES), jnp.bfloat16),
         in_specs=[vmem] * (nb + 1),
         out_specs=vmem,
-        scratch_shapes=[pltpu.VMEM((tokens, LANES), jnp.bfloat16)] * 3
-        + [pltpu.VMEM((nb, here, LANES), jnp.float32)],
+        scratch_shapes=[
+            pltpu.VMEM((tokens, LANES), jnp.bfloat16),
+            pltpu.VMEM((tokens, LANES), jnp.bfloat16),
+            pltpu.VMEM((head_dim + ONES, tokens), jnp.bfloat16),
+            pltpu.VMEM((2, tokens, QGROUP * BLOCK), jnp.float32),
+            pltpu.VMEM((2, tokens, QGROUP * BLOCK), jnp.bfloat16),
+            pltpu.VMEM((nb, here, LANES), jnp.float32),
+        ],
         cost_estimate=pl.CostEstimate(
             flops=4 * tokens * tokens // 2 * LANES,
             bytes_accessed=4 * tokens * LANES * 2,

time: 49.7 us -> 48.8 us (0.982)
  Pallas kernels: 7.66 us -> 6.7 us
    pallas_call x1, Pallas kernels: 4.54 us -> 3.62 us  [by_head(): pl.pallas_call(functools.partial(attend_kernel, nb, head_dim ** (-0.5)),...]
where the time goes in v3:
time: 48.8 us; the launch traced here: 48.5 us
  waiting for transfers between devices  18.6 us (38%)
  blocking collectives  12.6 us (26%)
  starting transfers between devices  10.6 us (22%)
  Pallas kernels  6.7 us (14%)
    all_to_all x1, waiting for transfers between devices, by_head(): whole = lax.all_to_all(packed, EVERY, split_axis=0, concat_axis=0)  16.1 us
    all_to_all x1, blocking collectives, by_head(): back = lax.all_to_all(attended, EVERY, split_axis=0, concat_axis=0)  12.6 us
    all_to_all x1, starting transfers between devices, by_head(): whole = lax.all_to_all(packed, EVERY, split_axis=0, concat_axis=0)  7.33 us
    pallas_call x1, Pallas kernels, by_head(): pl.pallas_call(functools.partial(attend_kernel, nb, head_dim ** (-0.5)),...  3.62 us
    ppermute x3, starting transfers between devices, by_head(): lax.ppermute(bias[step], 'blk', [(i, (i + step) % nb) for i in range(nb)])  3.28 us
    ppermute x3, waiting for transfers between devices, by_head(): lax.ppermute(bias[step], 'blk', [(i, (i + step) % nb) for i in range(nb)])  2.43 us
    pallas_call x1, Pallas kernels, by_head(): pl.pallas_call(functools.partial(pack_kernel, nu, nb), out_shape=(jax.Sha...  2.23 us
  transfers between devices with their start and end apart: 4, of which 3 were waited for; matrix products, arithmetic and copies ran while one was open for 0% of the time, Pallas kernels for 0%

profile of v3, /device:TPU:0, one launch (start us, length us, event | category | flops | bytes accessed | tf_op | source)
XLA Modules:
  0.0 48.5 jit_solution(3505772637428095108)
XLA Ops:
  0.0 2.2 %shard_map.46 = (bf16[4,8,96,128]{3,2,1,0:T(8,128)(2,1)}, f32[4,128]{1,0:T(4,128)S(1)}, f32[4,128]{1,0:T(4,128)S(1)}, f32[4,128]{1,0:T(4,128)S(1)}, f32[4,128]{1,0:T(4,128)S(1)}) custom-call(bf16[64,2048]{1,0:T(8,128)(2,1)} %q_hbm.1, bf16[64,2048]{1,0:T(8,128)(2,1)} %k_hbm.1, bf16[64,2048]{1,0:T(8,128)(2,1)} %v_hbm.1, s32[16,16]{1,0:T(8,128)} %bitcast.3), custom_call_target="tpu_custom_call" | custom-call | flops 524288 | bytes 1572864 | tf_op jit(solution)/shard_map/pallas_call | solution.py:263
  2.2 7.3 %all-to-all-start = ((bf16[32,96,128]{2,1,0:T(8,128)(2,1)}), bf16[32,96,128]{2,1,0:T(8,128)(2,1)S(1)}, u32[]{:S(2)}, u32[]{:S(2)}) async-start(bf16[32,96,128]{2,1,0:T(8,128)(2,1)} %bitcast.2), calls=%async_computation | async-start | bytes 1572864 | tf_op jit(solution)/shard_map/all_to_all | solution.py:283
  9.6 0.3 collective-permute-start
  9.9 1.6 %collective-permute-start.1 = (f32[4,128]{1,0:T(4,128)S(1)}, f32[4,128]{1,0:T(4,128)S(1)}, u32[]{:S(2)}, u32[]{:S(2)}) collective-permute-start(f32[4,128]{1,0:T(4,128)S(1)} %get-tuple-element.13), channel_id=1, source_target_pairs={{0,2},{1,3},{2,0},{3,1},{4,6},{5,7},{6,4},{7,5},{8,10},{9,11},{10,... | collective-permute-start | bytes 6152 | tf_op jit(solution)/shard_map/ppermute | solution.py:285
  11.5 1.4 %collective-permute-start.2 = (f32[4,128]{1,0:T(4,128)S(1)}, f32[4,128]{1,0:T(4,128)S(1)}, u32[]{:S(2)}, u32[]{:S(2)}) collective-permute-start(f32[4,128]{1,0:T(4,128)S(1)} %get-tuple-element.14), channel_id=1, source_target_pairs={{0,3},{1,0},{2,1},{3,2},{4,7},{5,4},{6,5},{7,6},{8,11},{9,8},{10,9... | collective-permute-start | bytes 6152 | tf_op jit(solution)/shard_map/ppermute | solution.py:285
  12.9 1.6 %collective-permute-done.rest_1_ = f32[4,128]{1,0:T(4,128)S(1)} collective-permute-done((f32[4,128]{1,0:T(4,128)S(1)}, f32[4,128]{1,0:T(4,128)S(1)}, u32[]{:S(2)}, u32[]{:S(2)}) %collective-permute-start) | collective-permute-done | bytes 2080 | tf_op jit(solution)/shard_map/ppermute | solution.py:285
  14.5 0.8 %collective-permute-done.1.rest_2_ = f32[4,128]{1,0:T(4,128)S(1)} collective-permute-done((f32[4,128]{1,0:T(4,128)S(1)}, f32[4,128]{1,0:T(4,128)S(1)}, u32[]{:S(2)}, u32[]{:S(2)}) %collective-permute-start.1) | collective-permute-done | bytes 2080 | tf_op jit(solution)/shard_map/ppermute | solution.py:285
  15.3 0.0 collective-permute-done.2.rest_3_
  15.3 16.1 %all-to-all-done.g_ref = bf16[32,96,128]{2,1,0:T(8,128)(2,1)S(1)} async-done(((bf16[32,96,128]{2,1,0:T(8,128)(2,1)}), bf16[32,96,128]{2,1,0:T(8,128)(2,1)S(1)}, u32[]{:S(2)}, u32[]{:S(2)}) %all-to-all-start) | async-done | bytes 786464 | tf_op jit(solution)/shard_map/all_to_all | solution.py:283
  31.4 3.6 %shard_map.47 = bf16[32,32,128]{2,1,0:T(8,128)(2,1)S(1)} custom-call(bf16[32,96,128]{2,1,0:T(8,128)(2,1)S(1)} %all-to-all-done.g_ref, f32[4,128]{1,0:T(4,128)S(1)} %get-tuple-element.11.rest_0_, f32[4,128]{1,0:T(4,128)S(1)} %collective-permute-done.rest_1_, f32[4,128]{1,0:T(4,128)S(1)} %collective-permute-done.1.rest_2_, ...), custom_call_target="tpu_custom_call" | custom-call | flops 1073741824 | bytes 2097152 | tf_op jit(solution)/shard_map/pallas_call | solution.py:289
  35.1 12.6 %all_to_all.10.g_ref = bf16[32,32,128]{2,1,0:T(8,128)(2,1)S(1)} all-to-all(bf16[32,32,128]{2,1,0:T(8,128)(2,1)S(1)} %shard_map.47), channel_id=1, replica_groups=mesh['uly'=8,'blk'=4] {'blk','uly'}, dimensions={0} | all-to-all | bytes 524288 | tf_op jit(solution)/shard_map/all_to_all | solution.py:308
  47.7 0.8 %shard_map.48 = bf16[64,2048]{1,0:T(8,128)(2,1)} custom-call(bf16[32,32,128]{2,1,0:T(8,128)(2,1)S(1)} %all_to_all.10.g_ref), custom_call_target="tpu_custom_call" | custom-call | flops 262144 | bytes 524288 | tf_op jit(solution)/shard_map/pallas_call | solution.py:309
Async XLA Ops:
  2.2 29.2 %all-to-all-start = ((bf16[32,96,128]{2,1,0:T(8,128)(2,1)}), bf16[32,96,128]{2,1,0:T(8,128)(2,1)S(1)}, u32[]{:S(2)}, u32[]{:S(2)}) async-start(bf16[32,96,128]{2,1,0:T(8,128)(2,1)} %bitcast.2), calls=%async_computation | async-start | bytes 1572864 | tf_op jit(solution)/shard_map/all_to_all | solution.py:283
  9.6 4.9 %collective-permute-start = (f32[4,128]{1,0:T(4,128)S(1)}, f32[4,128]{1,0:T(4,128)S(1)}, u32[]{:S(2)}, u32[]{:S(2)}) collective-permute-start(f32[4,128]{1,0:T(4,128)S(1)} %get-tuple-element.12), channel_id=1, source_target_pairs={{0,1},{1,2},{2,3},{3,0},{4,5},{5,6},{6,7},{7,4},{8,9},{9,10},{10,1... | collective-permute-start | bytes 6152 | tf_op jit(solution)/shard_map/ppermute | solution.py:285
  9.9 5.4 %collective-permute-start.1 = (f32[4,128]{1,0:T(4,128)S(1)}, f32[4,128]{1,0:T(4,128)S(1)}, u32[]{:S(2)}, u32[]{:S(2)}) collective-permute-start(f32[4,128]{1,0:T(4,128)S(1)} %get-tuple-element.13), channel_id=1, source_target_pairs={{0,2},{1,3},{2,0},{3,1},{4,6},{5,7},{6,4},{7,5},{8,10},{9,11},{10,... | collective-permute-start | bytes 6152 | tf_op jit(solution)/shard_map/ppermute | solution.py:285
  11.5 3.8 %collective-permute-start.2 = (f32[4,128]{1,0:T(4,128)S(1)}, f32[4,128]{1,0:T(4,128)S(1)}, u32[]{:S(2)}, u32[]{:S(2)}) collective-permute-start(f32[4,128]{1,0:T(4,128)S(1)} %get-tuple-element.14), channel_id=1, source_target_pairs={{0,3},{1,0},{2,1},{3,2},{4,7},{5,4},{6,5},{7,6},{8,11},{9,8},{10,9... | collective-permute-start | bytes 6152 | tf_op jit(solution)/shard_map/ppermute | solution.py:285

commit v4 on v3

--- a/solution.py
+++ b/solution.py
@@ -13,6 +13,7 @@
 LANES = 128
 NEG = -1e30
 ONES = 16
+AHEAD = 2
 PIECES = 4
 EVERY = ("blk", "uly")
 
@@ -205,9 +206,13 @@
     def weigh(slot, c, top):
         s = st[slot, c * group : (c + 1) * group, :]
         pt[slot, c * group : (c + 1) * group, :] = jnp.exp2((s - top) * factor).astype(jnp.bfloat16)
-    def finish(slot, g):
-        n = (g + 1) * group
-        total = jnp.dot(vt[:, :n], pt[slot, :n, :], preferred_element_type=jnp.float32)
+    def gather(slot, c0, c1, total):
+        part = jnp.dot(
+            vt[:, c0 * group : c1 * group], pt[slot, c0 * group : c1 * group, :],
+            preferred_element_type=jnp.float32,
+        )
+        return part if total is None else total + part
+    def finish(g, total):
         result = total[ones:] / total[:1]
         pair = jnp.concatenate([result[:, :mid], result[:, mid:]], axis=0)
         out_ref[g * each : (g + 1) * each] = pair.T.astype(jnp.bfloat16).reshape(each, half, LANES)
@@ -217,20 +222,27 @@
             if i not in ready:
                 ready.add(i); prepare(i)
     n = blocks // QGROUP
-    order = list(range(n))
-    prev = None
-    for i, g in enumerate(list(order) + [None]):
-        slot = i % 2
+    order = list(range(1, n, 2)) + list(range(0, n, 2))[::-1]
+    tops, slots = {}, AHEAD + 1
+    for i in range(n + AHEAD):
+        g = order[i] if i < n else None
+        w = order[i - AHEAD] if i >= AHEAD else None
         a = [] if g is None else list(range(g + 1))
-        b = [] if prev is None else list(range(prev[0] + 1))
+        b = [] if w is None else list(range(w + 1))
         if g is not None: need(g)
-        top = None
+        top, total, done = None, None, 0
+        k = 0
         for j in range(max(len(a), len(b))):
-            if j < len(a): top = score(slot, g, a[j], top)
-            if j < len(b): weigh(1 - slot, b[j], prev[1])
-        if prev is not None: finish(1 - slot, prev[0])
+            while k < len(b) and (not a or k * len(a) <= j * len(b)):
+                weigh((i - AHEAD) % slots, b[k], tops[w])
+                k += 1
+            if j < len(a): top = score(i % slots, g, a[j], top)
+        while k < len(b):
+            weigh((i - AHEAD) % slots, b[k], tops[w]); k += 1
         if g is not None:
-            prev = (g, jnp.max(top, axis=0, keepdims=True))
+            tops[g] = jnp.max(top, axis=0, keepdims=True)
+        if w is not None:
+            finish(w, gather((i - AHEAD) % slots, 0, w + 1, None))
 
 
 def unpack_kernel(nu, nb, g_ref, out_ref):
@@ -295,8 +307,8 @@
             pltpu.VMEM((tokens, LANES), jnp.bfloat16),
             pltpu.VMEM((tokens, LANES), jnp.bfloat16),
             pltpu.VMEM((head_dim + ONES, tokens), jnp.bfloat16),
-            pltpu.VMEM((2, tokens, QGROUP * BLOCK), jnp.float32),
-            pltpu.VMEM((2, tokens, QGROUP * BLOCK), jnp.bfloat16),
+            pltpu.VMEM((AHEAD + 1, tokens, QGROUP * BLOCK), jnp.float32),
+            pltpu.VMEM((AHEAD + 1, tokens, QGROUP * BLOCK), jnp.bfloat16),
             pltpu.VMEM((nb, here, LANES), jnp.float32),
         ],
         cost_estimate=pl.CostEstimate(

time: 48.8 us -> 48.2 us (0.988)
  Pallas kernels: 6.7 us -> 6.15 us
    pallas_call x1, Pallas kernels: 3.62 us -> 3.07 us  [by_head(): pl.pallas_call(functools.partial(attend_kernel, nb, head_dim ** (-0.5)),...]
where the time goes in v4:
time: 48.2 us; the launch traced here: 48 us
  waiting for transfers between devices  18.6 us (39%)
  blocking collectives  12.6 us (26%)
  starting transfers between devices  10.6 us (22%)
  Pallas kernels  6.15 us (13%)
    all_to_all x1, waiting for transfers between devices, by_head(): whole = lax.all_to_all(packed, EVERY, split_axis=0, concat_axis=0)  16.1 us
    all_to_all x1, blocking collectives, by_head(): back = lax.all_to_all(attended, EVERY, split_axis=0, concat_axis=0)  12.6 us
    all_to_all x1, starting transfers between devices, by_head(): whole = lax.all_to_all(packed, EVERY, split_axis=0, concat_axis=0)  7.33 us
    ppermute x3, starting transfers between devices, by_head(): lax.ppermute(bias[step], 'blk', [(i, (i + step) % nb) for i in range(nb)])  3.28 us
    pallas_call x1, Pallas kernels, by_head(): pl.pallas_call(functools.partial(attend_kernel, nb, head_dim ** (-0.5)),...  3.07 us
    ppermute x3, waiting for transfers between devices, by_head(): lax.ppermute(bias[step], 'blk', [(i, (i + step) % nb) for i in range(nb)])  2.43 us
    pallas_call x1, Pallas kernels, by_head(): pl.pallas_call(functools.partial(pack_kernel, nu, nb), out_shape=(jax.Sha...  2.23 us
  transfers between devices with their start and end apart: 4, of which 3 were waited for; matrix products, arithmetic and copies ran while one was open for 0% of the time, Pallas kernels for 0%

profile of v4, /device:TPU:0, one launch (start us, length us, event | category | flops | bytes accessed | tf_op | source)
XLA Modules:
  0.0 48.0 jit_solution(1283548208759103006)
XLA Ops:
  0.0 2.2 %shard_map.46 = (bf16[4,8,96,128]{3,2,1,0:T(8,128)(2,1)}, f32[4,128]{1,0:T(4,128)S(1)}, f32[4,128]{1,0:T(4,128)S(1)}, f32[4,128]{1,0:T(4,128)S(1)}, f32[4,128]{1,0:T(4,128)S(1)}) custom-call(bf16[64,2048]{1,0:T(8,128)(2,1)} %q_hbm.1, bf16[64,2048]{1,0:T(8,128)(2,1)} %k_hbm.1, bf16[64,2048]{1,0:T(8,128)(2,1)} %v_hbm.1, s32[16,16]{1,0:T(8,128)} %bitcast.3), custom_call_target="tpu_custom_call" | custom-call | flops 524288 | bytes 1572864 | tf_op jit(solution)/shard_map/pallas_call | solution.py:275
  2.2 7.3 %all-to-all-start = ((bf16[32,96,128]{2,1,0:T(8,128)(2,1)}), bf16[32,96,128]{2,1,0:T(8,128)(2,1)S(1)}, u32[]{:S(2)}, u32[]{:S(2)}) async-start(bf16[32,96,128]{2,1,0:T(8,128)(2,1)} %bitcast.2), calls=%async_computation | async-start | bytes 1572864 | tf_op jit(solution)/shard_map/all_to_all | solution.py:295
  9.6 0.3 collective-permute-start
  9.9 1.6 %collective-permute-start.1 = (f32[4,128]{1,0:T(4,128)S(1)}, f32[4,128]{1,0:T(4,128)S(1)}, u32[]{:S(2)}, u32[]{:S(2)}) collective-permute-start(f32[4,128]{1,0:T(4,128)S(1)} %get-tuple-element.13), channel_id=1, source_target_pairs={{0,2},{1,3},{2,0},{3,1},{4,6},{5,7},{6,4},{7,5},{8,10},{9,11},{10,... | collective-permute-start | bytes 6152 | tf_op jit(solution)/shard_map/ppermute | solution.py:297
  11.5 1.4 %collective-permute-start.2 = (f32[4,128]{1,0:T(4,128)S(1)}, f32[4,128]{1,0:T(4,128)S(1)}, u32[]{:S(2)}, u32[]{:S(2)}) collective-permute-start(f32[4,128]{1,0:T(4,128)S(1)} %get-tuple-element.14), channel_id=1, source_target_pairs={{0,3},{1,0},{2,1},{3,2},{4,7},{5,4},{6,5},{7,6},{8,11},{9,8},{10,9... | collective-permute-start | bytes 6152 | tf_op jit(solution)/shard_map/ppermute | solution.py:297
  12.9 1.6 %collective-permute-done.rest_1_ = f32[4,128]{1,0:T(4,128)S(1)} collective-permute-done((f32[4,128]{1,0:T(4,128)S(1)}, f32[4,128]{1,0:T(4,128)S(1)}, u32[]{:S(2)}, u32[]{:S(2)}) %collective-permute-start) | collective-permute-done | bytes 2080 | tf_op jit(solution)/shard_map/ppermute | solution.py:297
  14.5 0.8 %collective-permute-done.1.rest_2_ = f32[4,128]{1,0:T(4,128)S(1)} collective-permute-done((f32[4,128]{1,0:T(4,128)S(1)}, f32[4,128]{1,0:T(4,128)S(1)}, u32[]{:S(2)}, u32[]{:S(2)}) %collective-permute-start.1) | collective-permute-done | bytes 2080 | tf_op jit(solution)/shard_map/ppermute | solution.py:297
  15.3 0.0 collective-permute-done.2.rest_3_
  15.3 16.1 %all-to-all-done.g_ref = bf16[32,96,128]{2,1,0:T(8,128)(2,1)S(1)} async-done(((bf16[32,96,128]{2,1,0:T(8,128)(2,1)}), bf16[32,96,128]{2,1,0:T(8,128)(2,1)S(1)}, u32[]{:S(2)}, u32[]{:S(2)}) %all-to-all-start) | async-done | bytes 786464 | tf_op jit(solution)/shard_map/all_to_all | solution.py:295
  31.4 3.1 %shard_map.47 = bf16[32,32,128]{2,1,0:T(8,128)(2,1)S(1)} custom-call(bf16[32,96,128]{2,1,0:T(8,128)(2,1)S(1)} %all-to-all-done.g_ref, f32[4,128]{1,0:T(4,128)S(1)} %get-tuple-element.11.rest_0_, f32[4,128]{1,0:T(4,128)S(1)} %collective-permute-done.rest_1_, f32[4,128]{1,0:T(4,128)S(1)} %collective-permute-done.1.rest_2_, ...), custom_call_target="tpu_custom_call" | custom-call | flops 1073741824 | bytes 2097152 | tf_op jit(solution)/shard_map/pallas_call | solution.py:301
  34.5 12.6 %all_to_all.10.g_ref = bf16[32,32,128]{2,1,0:T(8,128)(2,1)S(1)} all-to-all(bf16[32,32,128]{2,1,0:T(8,128)(2,1)S(1)} %shard_map.47), channel_id=1, replica_groups=mesh['uly'=8,'blk'=4] {'blk','uly'}, dimensions={0} | all-to-all | bytes 524288 | tf_op jit(solution)/shard_map/all_to_all | solution.py:320
  47.1 0.8 %shard_map.48 = bf16[64,2048]{1,0:T(8,128)(2,1)} custom-call(bf16[32,32,128]{2,1,0:T(8,128)(2,1)S(1)} %all_to_all.10.g_ref), custom_call_target="tpu_custom_call" | custom-call | flops 262144 | bytes 524288 | tf_op jit(solution)/shard_map/pallas_call | solution.py:321
Async XLA Ops:
  2.2 29.2 %all-to-all-start = ((bf16[32,96,128]{2,1,0:T(8,128)(2,1)}), bf16[32,96,128]{2,1,0:T(8,128)(2,1)S(1)}, u32[]{:S(2)}, u32[]{:S(2)}) async-start(bf16[32,96,128]{2,1,0:T(8,128)(2,1)} %bitcast.2), calls=%async_computation | async-start | bytes 1572864 | tf_op jit(solution)/shard_map/all_to_all | solution.py:295
  9.6 4.9 %collective-permute-start = (f32[4,128]{1,0:T(4,128)S(1)}, f32[4,128]{1,0:T(4,128)S(1)}, u32[]{:S(2)}, u32[]{:S(2)}) collective-permute-start(f32[4,128]{1,0:T(4,128)S(1)} %get-tuple-element.12), channel_id=1, source_target_pairs={{0,1},{1,2},{2,3},{3,0},{4,5},{5,6},{6,7},{7,4},{8,9},{9,10},{10,1... | collective-permute-start | bytes 6152 | tf_op jit(solution)/shard_map/ppermute | solution.py:297
  9.9 5.4 %collective-permute-start.1 = (f32[4,128]{1,0:T(4,128)S(1)}, f32[4,128]{1,0:T(4,128)S(1)}, u32[]{:S(2)}, u32[]{:S(2)}) collective-permute-start(f32[4,128]{1,0:T(4,128)S(1)} %get-tuple-element.13), channel_id=1, source_target_pairs={{0,2},{1,3},{2,0},{3,1},{4,6},{5,7},{6,4},{7,5},{8,10},{9,11},{10,... | collective-permute-start | bytes 6152 | tf_op jit(solution)/shard_map/ppermute | solution.py:297
  11.5 3.8 %collective-permute-start.2 = (f32[4,128]{1,0:T(4,128)S(1)}, f32[4,128]{1,0:T(4,128)S(1)}, u32[]{:S(2)}, u32[]{:S(2)}) collective-permute-start(f32[4,128]{1,0:T(4,128)S(1)} %get-tuple-element.14), channel_id=1, source_target_pairs={{0,3},{1,0},{2,1},{3,2},{4,7},{5,4},{6,5},{7,6},{8,11},{9,8},{10,9... | collective-permute-start | bytes 6152 | tf_op jit(solution)/shard_map/ppermute | solution.py:297

commit v5 on v4

--- a/solution.py
+++ b/solution.py
@@ -15,7 +15,7 @@
 ONES = 16
 AHEAD = 2
 PIECES = 4
-EVERY = ("blk", "uly")
+EVERY = ("uly", "blk")
 
 
 def head_major(token_rows, heads_local, head_dim):
@@ -85,18 +85,21 @@
     return lax.all_to_all(result, "uly", split_axis=0, concat_axis=1, tiled=True)
 
 
+def place(device, nu, nb):
+    u, b = divmod(device, nb)
+    return (u % 2 * (nu // 2) + u // 2) * nb + b
+
+
 def lane_of(shape):
     return lax.broadcasted_iota(jnp.int32, shape, len(shape) - 1)
 
 
-def pack_kernel(
-    nu, nb, q_hbm, k_hbm, v_hbm, list_hbm, out_hbm, *rest
-):
+def pack_kernel(nb, q_hbm, k_hbm, v_hbm, list_hbm, out_hbm, *rest):
     bias_refs, (qkv, listed, packed, bias, in_sems, out_sems, list_sem) = rest[:nb], rest[nb:]
     rows, width = q_hbm.shape
     half, hd = rows // 2, LANES // 2
     pieces = in_sems.shape[0]
-    wide, owners = width // pieces, nu // pieces
+    wide, part = width // pieces, out_hbm.shape[1] // pieces
     low = lane_of((rows, LANES)) < hd
     low_half = lane_of((half, LANES)) < hd
     reads, writes = [], []
@@ -123,16 +126,16 @@
             k_turned, v_turned = pltpu.roll(k, hd, 1), pltpu.roll(v, hd, 1)
             q_turned = pltpu.roll(q, hd, 1)
             for odd in range(2):
-                head = 2 * pair + odd
+                u, b = divmod(2 * pair + odd, nb)
                 if odd:
                     kv = jnp.where(low, k_turned, v)
                     qq = jnp.where(low_half, q_turned[:half], q[half:])
                 else:
                     kv = jnp.where(low, k, v_turned)
                     qq = jnp.where(low_half, q[:half], q_turned[half:])
-                packed[head % nb, head // nb, :rows, :] = kv
-                packed[head % nb, head // nb, rows:, :] = qq
-        some = pl.ds(piece * owners, owners)
+                packed[u % 2, u // 2, b, :rows, :] = kv
+                packed[u % 2, u // 2, b, rows:, :] = qq
+        some = pl.ds(piece * part, part)
         writes.append(
             pltpu.make_async_copy(packed.at[:, some], out_hbm.at[:, some], out_sems.at[piece])
         )
@@ -154,8 +157,8 @@
         copy.wait()
 
 
-def attend_kernel(nb, scale, g_ref, *rest):
-    bias_refs, (out_ref, qx, kx, vt, st, pt, bias) = rest[:nb], rest[nb:]
+def attend_kernel(nu, nb, scale, g_ref, *rest):
+    bias_refs, (out_ref, qx, kx, vt, bias) = rest[:nb], rest[nb:]
     chunks, packed, _ = g_ref.shape
     rows = packed * 2 // 3
     half, hd = rows // 2, LANES // 2
@@ -172,11 +175,15 @@
     mid = group // 2
     ones = vt.shape[0] - hd
     vt[:ones, :] = jnp.ones((ones, vt.shape[1]), jnp.bfloat16)
+
+    def owner(t):
+        return place(t % nu * nb + t // nu, nu, nb)
+
     def prepare(g):
         for t in range(g * each, (g + 1) * each):
             b = t * rows // BLOCK
-            kv = g_ref[t, :rows, :]
-            q = g_ref[t, rows:, :]
+            kv = g_ref[owner(t), :rows, :]
+            q = g_ref[owner(t), rows:, :]
             row = jnp.broadcast_to(bias[b // here, b % here : b % here + 1, :], (half, LANES))
             row = row.astype(jnp.bfloat16)
             kx[t * rows : (t + 1) * rows, :] = jnp.where(low, kv, (lane == hd + b).astype(jnp.bfloat16))
@@ -184,38 +191,44 @@
             qx[at : at + half, :] = jnp.where(low_half, q, row)
             qx[at + mid : at + mid + half, :] = jnp.where(low_half, pltpu.roll(q, hd, 1), row)
         for b in range(g * QGROUP, (g + 1) * QGROUP):
-            pair = jnp.concatenate([g_ref[b * BLOCK // rows + i, :rows, :] for i in range(BLOCK // rows)], axis=0)
+            pair = jnp.concatenate([g_ref[owner(b * BLOCK // rows + i), :rows, :] for i in range(BLOCK // rows)], axis=0)
             vt[ones:, b * BLOCK : (b + 1) * BLOCK] = pair.T[hd:, :]
     key = lax.broadcasted_iota(jnp.int32, (group, group), 0)
     col = lax.broadcasted_iota(jnp.int32, (group, group), 1)
     token = col % mid // half * rows + col // mid * half + col % half
     later = key > token
     factor = scale * math.log2(math.e)
-    def score(slot, g, c, top):
+    held = {}
+    def score(slot, g, c, e, top):
         s = lax.dot_general(
-            kx[c * group : (c + 1) * group, :],
+            kx[c * group : e * group, :],
             qx[g * group : (g + 1) * group, :],
             (((1,), (1,)), ((), ())),
             preferred_element_type=jnp.float32,
         )
-        if c == g:
-            s = jnp.where(later, NEG, s)
-        st[slot, c * group : (c + 1) * group, :] = s
-        m = jnp.max(s.reshape(group // 8, 8, group), axis=0)
-        return m if top is None else jnp.maximum(top, m)
+        for t in range(c, e):
+            tile = s[(t - c) * group : (t - c + 1) * group]
+            if t == g:
+                tile = jnp.where(later, NEG, tile)
+            held[slot, t] = tile
+            m = jnp.max(tile.reshape(group // 8, 8, group), axis=0)
+            top = m if top is None else jnp.maximum(top, m)
+        return top
     def weigh(slot, c, top):
-        s = st[slot, c * group : (c + 1) * group, :]
-        pt[slot, c * group : (c + 1) * group, :] = jnp.exp2((s - top) * factor).astype(jnp.bfloat16)
+        s = held[slot, c]
+        held[slot, c] = jnp.exp2((s - top) * factor).astype(jnp.bfloat16)
     def gather(slot, c0, c1, total):
         part = jnp.dot(
-            vt[:, c0 * group : c1 * group], pt[slot, c0 * group : c1 * group, :],
+            vt[:, c0 * group : c1 * group], jnp.concatenate([held[slot, x] for x in range(c0, c1)], axis=0),
             preferred_element_type=jnp.float32,
         )
         return part if total is None else total + part
     def finish(g, total):
-        result = total[ones:] / total[:1]
+        result = (total[ones:].reshape(hd // 8, 8, group) * (1.0 / total[:8])[None]).reshape(hd, group)
         pair = jnp.concatenate([result[:, :mid], result[:, mid:]], axis=0)
-        out_ref[g * each : (g + 1) * each] = pair.T.astype(jnp.bfloat16).reshape(each, half, LANES)
+        chunk = pair.T.astype(jnp.bfloat16)
+        for i in range(each):
+            out_ref[owner(g * each + i)] = chunk[i * half : (i + 1) * half]
     ready = set()
     def need(g):
         for i in range(g + 1):
@@ -236,7 +249,8 @@
             while k < len(b) and (not a or k * len(a) <= j * len(b)):
                 weigh((i - AHEAD) % slots, b[k], tops[w])
                 k += 1
-            if j < len(a): top = score(i % slots, g, a[j], top)
+            if j < len(a) and j % 2 == 0:
+                top = score(i % slots, g, j, min(j + 2, len(a)), top)
         while k < len(b):
             weigh((i - AHEAD) % slots, b[k], tops[w]); k += 1
         if g is not None:
@@ -250,11 +264,14 @@
     low = lane_of((half, LANES)) < hd
     for pair in range(out_ref.shape[1] // LANES):
         cols = slice(pair * LANES, (pair + 1) * LANES)
-        even, odd = 2 * pair, 2 * pair + 1
-        a = g_ref[(even % nb) * nu + even // nb]
-        b = g_ref[(odd % nb) * nu + odd // nb]
+        a, b = (g_ref[place(2 * pair + odd, nu, nb)] for odd in range(2))
         out_ref[:half, cols] = jnp.where(low, a, pltpu.roll(b, hd, 1))
         out_ref[half:, cols] = jnp.where(low, pltpu.roll(a, hd, 1), b)
+
+
+def exchange(chunks, nu, nb):
+    order = [u * nb + b for odd in range(2) for u in range(odd, nu, 2) for b in range(nb)]
+    return lax.all_to_all(chunks, EVERY, split_axis=0, concat_axis=0, axis_index_groups=[order])
 
 
 def in_vmem(x):
@@ -271,17 +288,18 @@
     vmem = pl.BlockSpec(memory_space=pltpu.VMEM)
     small = pltpu.VMEM((here, LANES), jnp.float32)
     anywhere = pl.BlockSpec(memory_space=pl.ANY)
-    pieces = math.gcd(nu, PIECES)
+    pieces = math.gcd(nu // 2, PIECES)
+    laid = (2, nu // 2, nb, rows * 3 // 2, LANES)
     packed, *bias = pl.pallas_call(
-        functools.partial(pack_kernel, nu, nb),
-        out_shape=(jax.ShapeDtypeStruct((nb, nu, rows * 3 // 2, LANES), jnp.bfloat16),)
+        functools.partial(pack_kernel, nb),
+        out_shape=(jax.ShapeDtypeStruct(laid, jnp.bfloat16),)
         + (small,) * nb,
         in_specs=[anywhere] * 4,
         out_specs=(anywhere,) + (vmem,) * nb,
         scratch_shapes=[
             pltpu.VMEM((3, rows, width), jnp.bfloat16),
             pltpu.VMEM((heads_local * here, slots), jnp.int32),
-            pltpu.VMEM((nb, nu, rows * 3 // 2, LANES), jnp.bfloat16),
+            pltpu.VMEM(laid, jnp.bfloat16),
             pltpu.VMEM((nb, here, LANES), jnp.float32),
             pltpu.SemaphoreType.DMA((pieces, 3)),
             pltpu.SemaphoreType.DMA((pieces,)),
@@ -291,15 +309,14 @@
             flops=4 * rows * width, bytes_accessed=12 * rows * width, transcendentals=0
         ),
     )(queries, keys, values, block_list.reshape(heads_local * here, slots))
-    packed = packed.reshape(count, rows * 3 // 2, LANES)
-    whole = lax.all_to_all(packed, EVERY, split_axis=0, concat_axis=0)
+    whole = exchange(packed.reshape(count, rows * 3 // 2, LANES), nu, nb)
     moved = [bias[0]] + [
         lax.ppermute(bias[step], "blk", [(i, (i + step) % nb) for i in range(nb)])
         for step in range(1, nb)
     ]
     tokens = count * rows
     attended = pl.pallas_call(
-        functools.partial(attend_kernel, nb, head_dim**-0.5),
+        functools.partial(attend_kernel, nu, nb, head_dim**-0.5),
         out_shape=pltpu.VMEM((count, rows // 2, LANES), jnp.bfloat16),
         in_specs=[vmem] * (nb + 1),
         out_specs=vmem,
@@ -307,8 +324,6 @@
             pltpu.VMEM((tokens, LANES), jnp.bfloat16),
             pltpu.VMEM((tokens, LANES), jnp.bfloat16),
             pltpu.VMEM((head_dim + ONES, tokens), jnp.bfloat16),
-            pltpu.VMEM((AHEAD + 1, tokens, QGROUP * BLOCK), jnp.float32),
-            pltpu.VMEM((AHEAD + 1, tokens, QGROUP * BLOCK), jnp.bfloat16),
             pltpu.VMEM((nb, here, LANES), jnp.float32),
         ],
         cost_estimate=pl.CostEstimate(
@@ -317,7 +332,7 @@
             transcendentals=tokens * tokens // 2,
         ),
     )(*(in_vmem(x) for x in (whole, *moved)))
-    back = lax.all_to_all(attended, EVERY, split_axis=0, concat_axis=0)
+    back = exchange(attended, nu, nb)
     return pl.pallas_call(
         functools.partial(unpack_kernel, nu, nb),
         out_shape=jax.ShapeDtypeStruct((rows, width), jnp.bfloat16),
@@ -337,6 +352,7 @@
     blocks = here * nb
     one_head = (
         heads_local == nb
+        and nu % 2 == 0
         and 2 * head_dim == LANES
         and blocks <= LANES // 2
         and blocks % QGROUP == 0

time: 48.2 us -> 47.6 us (0.988)
  no operation moved by 1% of the time
where the time goes in v5:
time: 47.6 us; the launch traced here: 47.3 us
  waiting for transfers between devices  18.2 us (38%)
  blocking collectives  12.2 us (26%)
  starting transfers between devices  10.6 us (22%)
  Pallas kernels  6.23 us (13%)
    all_to_all x1, waiting for transfers between devices, exchange(): lax.all_to_all(chunks, EVERY, split_axis=0, concat_axis=0, axis_index_gro...  15.8 us
    all_to_all x1, blocking collectives, exchange(): lax.all_to_all(chunks, EVERY, split_axis=0, concat_axis=0, axis_index_gro...  12.2 us
    all_to_all x1, starting transfers between devices, exchange(): lax.all_to_all(chunks, EVERY, split_axis=0, concat_axis=0, axis_index_gro...  7.33 us
    ppermute x3, starting transfers between devices, by_head(): lax.ppermute(bias[step], 'blk', [(i, (i + step) % nb) for i in range(nb)])  3.28 us
    pallas_call x1, Pallas kernels, by_head(): pl.pallas_call(functools.partial(attend_kernel, nu, nb, head_dim ** (-0.5...  3.16 us
    ppermute x3, waiting for transfers between devices, by_head(): lax.ppermute(bias[step], 'blk', [(i, (i + step) % nb) for i in range(nb)])  2.41 us
    pallas_call x1, Pallas kernels, by_head(): pl.pallas_call(functools.partial(pack_kernel, nb), out_shape=(jax.ShapeDt...  2.23 us
  transfers between devices with their start and end apart: 4, of which 3 were waited for; matrix products, arithmetic and copies ran while one was open for 0% of the time, Pallas kernels for 0%

profile of v5, /device:TPU:0, one launch (start us, length us, event | category | flops | bytes accessed | tf_op | source)
XLA Modules:
  0.0 47.3 jit_solution(11003478100755690523)
XLA Ops:
  0.0 2.2 %shard_map.46 = (bf16[2,4,4,96,128]{4,3,2,1,0:T(8,128)(2,1)}, f32[4,128]{1,0:T(4,128)S(1)}, f32[4,128]{1,0:T(4,128)S(1)}, f32[4,128]{1,0:T(4,128)S(1)}, f32[4,128]{1,0:T(4,128)S(1)}) custom-call(bf16[64,2048]{1,0:T(8,128)(2,1)} %q_hbm.1, bf16[64,2048]{1,0:T(8,128)(2,1)} %k_hbm.1, bf16[64,2048]{1,0:T(8,128)(2,1)} %v_hbm.1, s32[16,16]{1,0:T(8,128)} %bitcast.3), custom_call_target="tpu_custom_call" | custom-call | flops 524288 | bytes 1572864 | tf_op jit(solution)/shard_map/pallas_call | solution.py:293
  2.2 7.3 %all-to-all-start = ((bf16[32,96,128]{2,1,0:T(8,128)(2,1)}), bf16[32,96,128]{2,1,0:T(8,128)(2,1)S(1)}, u32[]{:S(2)}, u32[]{:S(2)}) async-start(bf16[32,96,128]{2,1,0:T(8,128)(2,1)} %bitcast.2), calls=%async_computation | async-start | bytes 1572864 | tf_op jit(solution)/shard_map/all_to_all | solution.py:274
  9.6 0.3 collective-permute-start
  9.9 1.6 %collective-permute-start.1 = (f32[4,128]{1,0:T(4,128)S(1)}, f32[4,128]{1,0:T(4,128)S(1)}, u32[]{:S(2)}, u32[]{:S(2)}) collective-permute-start(f32[4,128]{1,0:T(4,128)S(1)} %get-tuple-element.13), channel_id=1, source_target_pairs={{0,2},{1,3},{2,0},{3,1},{4,6},{5,7},{6,4},{7,5},{8,10},{9,11},{10,... | collective-permute-start | bytes 6152 | tf_op jit(solution)/shard_map/ppermute | solution.py:314
  11.5 1.4 %collective-permute-start.2 = (f32[4,128]{1,0:T(4,128)S(1)}, f32[4,128]{1,0:T(4,128)S(1)}, u32[]{:S(2)}, u32[]{:S(2)}) collective-permute-start(f32[4,128]{1,0:T(4,128)S(1)} %get-tuple-element.14), channel_id=1, source_target_pairs={{0,3},{1,0},{2,1},{3,2},{4,7},{5,4},{6,5},{7,6},{8,11},{9,8},{10,9... | collective-permute-start | bytes 6152 | tf_op jit(solution)/shard_map/ppermute | solution.py:314
  12.9 1.3 %collective-permute-done.rest_1_ = f32[4,128]{1,0:T(4,128)S(1)} collective-permute-done((f32[4,128]{1,0:T(4,128)S(1)}, f32[4,128]{1,0:T(4,128)S(1)}, u32[]{:S(2)}, u32[]{:S(2)}) %collective-permute-start) | collective-permute-done | bytes 2080 | tf_op jit(solution)/shard_map/ppermute | solution.py:314
  14.2 1.1 %collective-permute-done.1.rest_2_ = f32[4,128]{1,0:T(4,128)S(1)} collective-permute-done((f32[4,128]{1,0:T(4,128)S(1)}, f32[4,128]{1,0:T(4,128)S(1)}, u32[]{:S(2)}, u32[]{:S(2)}) %collective-permute-start.1) | collective-permute-done | bytes 2080 | tf_op jit(solution)/shard_map/ppermute | solution.py:314
  15.3 0.0 collective-permute-done.2.rest_3_
  15.3 15.8 %all-to-all-done.g_ref = bf16[32,96,128]{2,1,0:T(8,128)(2,1)S(1)} async-done(((bf16[32,96,128]{2,1,0:T(8,128)(2,1)}), bf16[32,96,128]{2,1,0:T(8,128)(2,1)S(1)}, u32[]{:S(2)}, u32[]{:S(2)}) %all-to-all-start) | async-done | bytes 786464 | tf_op jit(solution)/shard_map/all_to_all | solution.py:274
  31.1 3.2 %shard_map.47 = bf16[32,32,128]{2,1,0:T(8,128)(2,1)S(1)} custom-call(bf16[32,96,128]{2,1,0:T(8,128)(2,1)S(1)} %all-to-all-done.g_ref, f32[4,128]{1,0:T(4,128)S(1)} %get-tuple-element.11.rest_0_, f32[4,128]{1,0:T(4,128)S(1)} %collective-permute-done.rest_1_, f32[4,128]{1,0:T(4,128)S(1)} %collective-permute-done.1.rest_2_, ...), custom_call_target="tpu_custom_call" | custom-call | flops 1073741824 | bytes 2097152 | tf_op jit(solution)/shard_map/pallas_call | solution.py:318
  34.3 12.2 %all_to_all.10.g_ref = bf16[32,32,128]{2,1,0:T(8,128)(2,1)S(1)} all-to-all(bf16[32,32,128]{2,1,0:T(8,128)(2,1)S(1)} %shard_map.47), channel_id=1, replica_groups={{0,1,2,3,8,9,10,11,16,17,18,19,24,25,26,27,4,5,6,7,12,13,14,15,20,21,22..., dimensions={0} | all-to-all | bytes 524288 | tf_op jit(solution)/shard_map/all_to_all | solution.py:274
  46.5 0.8 %shard_map.48 = bf16[64,2048]{1,0:T(8,128)(2,1)} custom-call(bf16[32,32,128]{2,1,0:T(8,128)(2,1)S(1)} %all_to_all.10.g_ref), custom_call_target="tpu_custom_call" | custom-call | flops 262144 | bytes 524288 | tf_op jit(solution)/shard_map/pallas_call | solution.py:336
Async XLA Ops:
  2.2 28.8 %all-to-all-start = ((bf16[32,96,128]{2,1,0:T(8,128)(2,1)}), bf16[32,96,128]{2,1,0:T(8,128)(2,1)S(1)}, u32[]{:S(2)}, u32[]{:S(2)}) async-start(bf16[32,96,128]{2,1,0:T(8,128)(2,1)} %bitcast.2), calls=%async_computation | async-start | bytes 1572864 | tf_op jit(solution)/shard_map/all_to_all | solution.py:274
  9.6 4.6 %collective-permute-start = (f32[4,128]{1,0:T(4,128)S(1)}, f32[4,128]{1,0:T(4,128)S(1)}, u32[]{:S(2)}, u32[]{:S(2)}) collective-permute-start(f32[4,128]{1,0:T(4,128)S(1)} %get-tuple-element.12), channel_id=1, source_target_pairs={{0,1},{1,2},{2,3},{3,0},{4,5},{5,6},{6,7},{7,4},{8,9},{9,10},{10,1... | collective-permute-start | bytes 6152 | tf_op jit(solution)/shard_map/ppermute | solution.py:314
  9.9 5.4 %collective-permute-start.1 = (f32[4,128]{1,0:T(4,128)S(1)}, f32[4,128]{1,0:T(4,128)S(1)}, u32[]{:S(2)}, u32[]{:S(2)}) collective-permute-start(f32[4,128]{1,0:T(4,128)S(1)} %get-tuple-element.13), channel_id=1, source_target_pairs={{0,2},{1,3},{2,0},{3,1},{4,6},{5,7},{6,4},{7,5},{8,10},{9,11},{10,... | collective-permute-start | bytes 6152 | tf_op jit(solution)/shard_map/ppermute | solution.py:314
  11.5 3.8 %collective-permute-start.2 = (f32[4,128]{1,0:T(4,128)S(1)}, f32[4,128]{1,0:T(4,128)S(1)}, u32[]{:S(2)}, u32[]{:S(2)}) collective-permute-start(f32[4,128]{1,0:T(4,128)S(1)} %get-tuple-element.14), channel_id=1, source_target_pairs={{0,3},{1,0},{2,1},{3,2},{4,7},{5,4},{6,5},{7,6},{8,11},{9,8},{10,9... | collective-permute-start | bytes 6152 | tf_op jit(solution)/shard_map/ppermute | solution.py:314

commit v6 on v5

--- a/solution.py
+++ b/solution.py
@@ -259,14 +259,25 @@
             finish(w, gather((i - AHEAD) % slots, 0, w + 1, None))
 
 
-def unpack_kernel(nu, nb, g_ref, out_ref):
+def unpack_kernel(nu, nb, g_ref, out_hbm, out, sems):
     half, hd = g_ref.shape[1], LANES // 2
     low = lane_of((half, LANES)) < hd
-    for pair in range(out_ref.shape[1] // LANES):
-        cols = slice(pair * LANES, (pair + 1) * LANES)
-        a, b = (g_ref[place(2 * pair + odd, nu, nb)] for odd in range(2))
-        out_ref[:half, cols] = jnp.where(low, a, pltpu.roll(b, hd, 1))
-        out_ref[half:, cols] = jnp.where(low, pltpu.roll(a, hd, 1), b)
+    pieces = sems.shape[0]
+    wide = out.shape[1] // pieces
+    writes = []
+    for piece in range(pieces):
+        for pair in range(piece * wide // LANES, (piece + 1) * wide // LANES):
+            cols = slice(pair * LANES, (pair + 1) * LANES)
+            a, b = (g_ref[place(2 * pair + odd, nu, nb)] for odd in range(2))
+            out[:half, cols] = jnp.where(low, a, pltpu.roll(b, hd, 1))
+            out[half:, cols] = jnp.where(low, pltpu.roll(a, hd, 1), b)
+        cols = pl.ds(piece * wide, wide)
+        writes.append(
+            pltpu.make_async_copy(out.at[:, cols], out_hbm.at[:, cols], sems.at[piece])
+        )
+        writes[-1].start()
+    for copy in writes:
+        copy.wait()
 
 
 def exchange(chunks, nu, nb):
@@ -337,7 +348,11 @@
         functools.partial(unpack_kernel, nu, nb),
         out_shape=jax.ShapeDtypeStruct((rows, width), jnp.bfloat16),
         in_specs=[vmem],
-        out_specs=vmem,
+        out_specs=anywhere,
+        scratch_shapes=[
+            pltpu.VMEM((rows, width), jnp.bfloat16),
+            pltpu.SemaphoreType.DMA((pieces,)),
+        ],
         cost_estimate=pl.CostEstimate(
             flops=2 * rows * width, bytes_accessed=4 * rows * width, transcendentals=0
         ),

time: 47.6 us -> 47.6 us (level)
  no operation moved by 1% of the time
where the time goes in v6:
time: 47.6 us; the launch traced here: 47.3 us
  waiting for transfers between devices  18.2 us (38%)
  blocking collectives  12.2 us (26%)
  starting transfers between devices  10.6 us (22%)
  Pallas kernels  6.21 us (13%)
    all_to_all x1, waiting for transfers between devices, exchange(): lax.all_to_all(chunks, EVERY, split_axis=0, concat_axis=0, axis_index_gro...  15.8 us
    all_to_all x1, blocking collectives, exchange(): lax.all_to_all(chunks, EVERY, split_axis=0, concat_axis=0, axis_index_gro...  12.2 us
    all_to_all x1, starting transfers between devices, exchange(): lax.all_to_all(chunks, EVERY, split_axis=0, concat_axis=0, axis_index_gro...  7.33 us
    ppermute x3, starting transfers between devices, by_head(): lax.ppermute(bias[step], 'blk', [(i, (i + step) % nb) for i in range(nb)])  3.28 us
    pallas_call x1, Pallas kernels, by_head(): pl.pallas_call(functools.partial(attend_kernel, nu, nb, head_dim ** (-0.5...  3.16 us
    ppermute x3, waiting for transfers between devices, by_head(): lax.ppermute(bias[step], 'blk', [(i, (i + step) % nb) for i in range(nb)])  2.41 us
    pallas_call x1, Pallas kernels, by_head(): pl.pallas_call(functools.partial(pack_kernel, nb), out_shape=(jax.ShapeDt...  2.23 us
  transfers between devices with their start and end apart: 4, of which 3 were waited for; matrix products, arithmetic and copies ran while one was open for 0% of the time, Pallas kernels for 0%

profile of v6, /device:TPU:0, one launch (start us, length us, event | category | flops | bytes accessed | tf_op | source)
XLA Modules:
  0.0 47.3 jit_solution(253188725911787561)
XLA Ops:
  0.0 2.2 %shard_map.46 = (bf16[2,4,4,96,128]{4,3,2,1,0:T(8,128)(2,1)}, f32[4,128]{1,0:T(4,128)S(1)}, f32[4,128]{1,0:T(4,128)S(1)}, f32[4,128]{1,0:T(4,128)S(1)}, f32[4,128]{1,0:T(4,128)S(1)}) custom-call(bf16[64,2048]{1,0:T(8,128)(2,1)} %q_hbm.1, bf16[64,2048]{1,0:T(8,128)(2,1)} %k_hbm.1, bf16[64,2048]{1,0:T(8,128)(2,1)} %v_hbm.1, s32[16,16]{1,0:T(8,128)} %bitcast.3), custom_call_target="tpu_custom_call" | custom-call | flops 524288 | bytes 1572864 | tf_op jit(solution)/shard_map/pallas_call | solution.py:304
  2.2 7.3 %all-to-all-start = ((bf16[32,96,128]{2,1,0:T(8,128)(2,1)}), bf16[32,96,128]{2,1,0:T(8,128)(2,1)S(1)}, u32[]{:S(2)}, u32[]{:S(2)}) async-start(bf16[32,96,128]{2,1,0:T(8,128)(2,1)} %bitcast.2), calls=%async_computation | async-start | bytes 1572864 | tf_op jit(solution)/shard_map/all_to_all | solution.py:285
  9.6 0.3 collective-permute-start
  9.9 1.6 %collective-permute-start.1 = (f32[4,128]{1,0:T(4,128)S(1)}, f32[4,128]{1,0:T(4,128)S(1)}, u32[]{:S(2)}, u32[]{:S(2)}) collective-permute-start(f32[4,128]{1,0:T(4,128)S(1)} %get-tuple-element.13), channel_id=1, source_target_pairs={{0,2},{1,3},{2,0},{3,1},{4,6},{5,7},{6,4},{7,5},{8,10},{9,11},{10,... | collective-permute-start | bytes 6152 | tf_op jit(solution)/shard_map/ppermute | solution.py:325
  11.5 1.4 %collective-permute-start.2 = (f32[4,128]{1,0:T(4,128)S(1)}, f32[4,128]{1,0:T(4,128)S(1)}, u32[]{:S(2)}, u32[]{:S(2)}) collective-permute-start(f32[4,128]{1,0:T(4,128)S(1)} %get-tuple-element.14), channel_id=1, source_target_pairs={{0,3},{1,0},{2,1},{3,2},{4,7},{5,4},{6,5},{7,6},{8,11},{9,8},{10,9... | collective-permute-start | bytes 6152 | tf_op jit(solution)/shard_map/ppermute | solution.py:325
  12.9 1.3 %collective-permute-done.rest_1_ = f32[4,128]{1,0:T(4,128)S(1)} collective-permute-done((f32[4,128]{1,0:T(4,128)S(1)}, f32[4,128]{1,0:T(4,128)S(1)}, u32[]{:S(2)}, u32[]{:S(2)}) %collective-permute-start) | collective-permute-done | bytes 2080 | tf_op jit(solution)/shard_map/ppermute | solution.py:325
  14.2 1.1 %collective-permute-done.1.rest_2_ = f32[4,128]{1,0:T(4,128)S(1)} collective-permute-done((f32[4,128]{1,0:T(4,128)S(1)}, f32[4,128]{1,0:T(4,128)S(1)}, u32[]{:S(2)}, u32[]{:S(2)}) %collective-permute-start.1) | collective-permute-done | bytes 2080 | tf_op jit(solution)/shard_map/ppermute | solution.py:325
  15.3 0.0 collective-permute-done.2.rest_3_
  15.3 15.8 %all-to-all-done.g_ref = bf16[32,96,128]{2,1,0:T(8,128)(2,1)S(1)} async-done(((bf16[32,96,128]{2,1,0:T(8,128)(2,1)}), bf16[32,96,128]{2,1,0:T(8,128)(2,1)S(1)}, u32[]{:S(2)}, u32[]{:S(2)}) %all-to-all-start) | async-done | bytes 786464 | tf_op jit(solution)/shard_map/all_to_all | solution.py:285
  31.1 3.2 %shard_map.47 = bf16[32,32,128]{2,1,0:T(8,128)(2,1)S(1)} custom-call(bf16[32,96,128]{2,1,0:T(8,128)(2,1)S(1)} %all-to-all-done.g_ref, f32[4,128]{1,0:T(4,128)S(1)} %get-tuple-element.11.rest_0_, f32[4,128]{1,0:T(4,128)S(1)} %collective-permute-done.rest_1_, f32[4,128]{1,0:T(4,128)S(1)} %collective-permute-done.1.rest_2_, ...), custom_call_target="tpu_custom_call" | custom-call | flops 1073741824 | bytes 2097152 | tf_op jit(solution)/shard_map/pallas_call | solution.py:329
  34.3 12.2 %all_to_all.10.g_ref = bf16[32,32,128]{2,1,0:T(8,128)(2,1)S(1)} all-to-all(bf16[32,32,128]{2,1,0:T(8,128)(2,1)S(1)} %shard_map.47), channel_id=1, replica_groups={{0,1,2,3,8,9,10,11,16,17,18,19,24,25,26,27,4,5,6,7,12,13,14,15,20,21,22..., dimensions={0} | all-to-all | bytes 524288 | tf_op jit(solution)/shard_map/all_to_all | solution.py:285
  46.5 0.8 %shard_map.48 = bf16[64,2048]{1,0:T(8,128)(2,1)} custom-call(bf16[32,32,128]{2,1,0:T(8,128)(2,1)S(1)} %all_to_all.10.g_ref), custom_call_target="tpu_custom_call" | custom-call | flops 262144 | bytes 524288 | tf_op jit(solution)/shard_map/pallas_call | solution.py:347
Async XLA Ops:
  2.2 28.8 %all-to-all-start = ((bf16[32,96,128]{2,1,0:T(8,128)(2,1)}), bf16[32,96,128]{2,1,0:T(8,128)(2,1)S(1)}, u32[]{:S(2)}, u32[]{:S(2)}) async-start(bf16[32,96,128]{2,1,0:T(8,128)(2,1)} %bitcast.2), calls=%async_computation | async-start | bytes 1572864 | tf_op jit(solution)/shard_map/all_to_all | solution.py:285
  9.6 4.6 %collective-permute-start = (f32[4,128]{1,0:T(4,128)S(1)}, f32[4,128]{1,0:T(4,128)S(1)}, u32[]{:S(2)}, u32[]{:S(2)}) collective-permute-start(f32[4,128]{1,0:T(4,128)S(1)} %get-tuple-element.12), channel_id=1, source_target_pairs={{0,1},{1,2},{2,3},{3,0},{4,5},{5,6},{6,7},{7,4},{8,9},{9,10},{10,1... | collective-permute-start | bytes 6152 | tf_op jit(solution)/shard_map/ppermute | solution.py:325
  9.9 5.4 %collective-permute-start.1 = (f32[4,128]{1,0:T(4,128)S(1)}, f32[4,128]{1,0:T(4,128)S(1)}, u32[]{:S(2)}, u32[]{:S(2)}) collective-permute-start(f32[4,128]{1,0:T(4,128)S(1)} %get-tuple-element.13), channel_id=1, source_target_pairs={{0,2},{1,3},{2,0},{3,1},{4,6},{5,7},{6,4},{7,5},{8,10},{9,11},{10,... | collective-permute-start | bytes 6152 | tf_op jit(solution)/shard_map/ppermute | solution.py:325
  11.5 3.8 %collective-permute-start.2 = (f32[4,128]{1,0:T(4,128)S(1)}, f32[4,128]{1,0:T(4,128)S(1)}, u32[]{:S(2)}, u32[]{:S(2)}) collective-permute-start(f32[4,128]{1,0:T(4,128)S(1)} %get-tuple-element.14), channel_id=1, source_target_pairs={{0,3},{1,0},{2,1},{3,2},{4,7},{5,4},{6,5},{7,6},{8,11},{9,8},{10,9... | collective-permute-start | bytes 6152 | tf_op jit(solution)/shard_map/ppermute | solution.py:325

commit v7 on v5

--- a/solution.py
+++ b/solution.py
@@ -14,7 +14,7 @@
 NEG = -1e30
 ONES = 16
 AHEAD = 2
-PIECES = 4
+PIECES = 2
 EVERY = ("uly", "blk")
 
 

time: 47.6 us -> 47.5 us (level)
  no operation moved by 1% of the time
where the time goes in v7:
time: 47.5 us; the launch traced here: 47.3 us
  waiting for transfers between devices  18.2 us (38%)
  blocking collectives  12.2 us (26%)
  starting transfers between devices  10.6 us (22%)
  Pallas kernels  6.2 us (13%)
    all_to_all x1, waiting for transfers between devices, exchange(): lax.all_to_all(chunks, EVERY, split_axis=0, concat_axis=0, axis_index_gro...  15.8 us
    all_to_all x1, blocking collectives, exchange(): lax.all_to_all(chunks, EVERY, split_axis=0, concat_axis=0, axis_index_gro...  12.2 us
    all_to_all x1, starting transfers between devices, exchange(): lax.all_to_all(chunks, EVERY, split_axis=0, concat_axis=0, axis_index_gro...  7.33 us
    ppermute x3, starting transfers between devices, by_head(): lax.ppermute(bias[step], 'blk', [(i, (i + step) % nb) for i in range(nb)])  3.28 us
    pallas_call x1, Pallas kernels, by_head(): pl.pallas_call(functools.partial(attend_kernel, nu, nb, head_dim ** (-0.5...  3.17 us
    ppermute x3, waiting for transfers between devices, by_head(): lax.ppermute(bias[step], 'blk', [(i, (i + step) % nb) for i in range(nb)])  2.41 us
    pallas_call x1, Pallas kernels, by_head(): pl.pallas_call(functools.partial(pack_kernel, nb), out_shape=(jax.ShapeDt...  2.19 us
  transfers between devices with their start and end apart: 4, of which 3 were waited for; matrix products, arithmetic and copies ran while one was open for 0% of the time, Pallas kernels for 0%

profile of v7, /device:TPU:0, one launch (start us, length us, event | category | flops | bytes accessed | tf_op | source)
XLA Modules:
  0.0 47.3 jit_solution(10287670161355447710)
XLA Ops:
  0.0 2.2 %shard_map.46 = (bf16[2,4,4,96,128]{4,3,2,1,0:T(8,128)(2,1)}, f32[4,128]{1,0:T(4,128)S(1)}, f32[4,128]{1,0:T(4,128)S(1)}, f32[4,128]{1,0:T(4,128)S(1)}, f32[4,128]{1,0:T(4,128)S(1)}) custom-call(bf16[64,2048]{1,0:T(8,128)(2,1)} %q_hbm.1, bf16[64,2048]{1,0:T(8,128)(2,1)} %k_hbm.1, bf16[64,2048]{1,0:T(8,128)(2,1)} %v_hbm.1, s32[16,16]{1,0:T(8,128)} %bitcast.3), custom_call_target="tpu_custom_call" | custom-call | flops 524288 | bytes 1572864 | tf_op jit(solution)/shard_map/pallas_call | solution.py:293
  2.2 7.3 %all-to-all-start = ((bf16[32,96,128]{2,1,0:T(8,128)(2,1)}), bf16[32,96,128]{2,1,0:T(8,128)(2,1)S(1)}, u32[]{:S(2)}, u32[]{:S(2)}) async-start(bf16[32,96,128]{2,1,0:T(8,128)(2,1)} %bitcast.2), calls=%async_computation | async-start | bytes 1572864 | tf_op jit(solution)/shard_map/all_to_all | solution.py:274
  9.5 0.3 collective-permute-start
  9.8 1.6 %collective-permute-start.1 = (f32[4,128]{1,0:T(4,128)S(1)}, f32[4,128]{1,0:T(4,128)S(1)}, u32[]{:S(2)}, u32[]{:S(2)}) collective-permute-start(f32[4,128]{1,0:T(4,128)S(1)} %get-tuple-element.13), channel_id=1, source_target_pairs={{0,2},{1,3},{2,0},{3,1},{4,6},{5,7},{6,4},{7,5},{8,10},{9,11},{10,... | collective-permute-start | bytes 6152 | tf_op jit(solution)/shard_map/ppermute | solution.py:314
  11.5 1.4 %collective-permute-start.2 = (f32[4,128]{1,0:T(4,128)S(1)}, f32[4,128]{1,0:T(4,128)S(1)}, u32[]{:S(2)}, u32[]{:S(2)}) collective-permute-start(f32[4,128]{1,0:T(4,128)S(1)} %get-tuple-element.14), channel_id=1, source_target_pairs={{0,3},{1,0},{2,1},{3,2},{4,7},{5,4},{6,5},{7,6},{8,11},{9,8},{10,9... | collective-permute-start | bytes 6152 | tf_op jit(solution)/shard_map/ppermute | solution.py:314
  12.8 1.3 %collective-permute-done.rest_1_ = f32[4,128]{1,0:T(4,128)S(1)} collective-permute-done((f32[4,128]{1,0:T(4,128)S(1)}, f32[4,128]{1,0:T(4,128)S(1)}, u32[]{:S(2)}, u32[]{:S(2)}) %collective-permute-start) | collective-permute-done | bytes 2080 | tf_op jit(solution)/shard_map/ppermute | solution.py:314
  14.1 1.1 %collective-permute-done.1.rest_2_ = f32[4,128]{1,0:T(4,128)S(1)} collective-permute-done((f32[4,128]{1,0:T(4,128)S(1)}, f32[4,128]{1,0:T(4,128)S(1)}, u32[]{:S(2)}, u32[]{:S(2)}) %collective-permute-start.1) | collective-permute-done | bytes 2080 | tf_op jit(solution)/shard_map/ppermute | solution.py:314
  15.2 0.0 collective-permute-done.2.rest_3_
  15.2 15.8 %all-to-all-done.g_ref = bf16[32,96,128]{2,1,0:T(8,128)(2,1)S(1)} async-done(((bf16[32,96,128]{2,1,0:T(8,128)(2,1)}), bf16[32,96,128]{2,1,0:T(8,128)(2,1)S(1)}, u32[]{:S(2)}, u32[]{:S(2)}) %all-to-all-start) | async-done | bytes 786464 | tf_op jit(solution)/shard_map/all_to_all | solution.py:274
  31.0 3.2 %shard_map.47 = bf16[32,32,128]{2,1,0:T(8,128)(2,1)S(1)} custom-call(bf16[32,96,128]{2,1,0:T(8,128)(2,1)S(1)} %all-to-all-done.g_ref, f32[4,128]{1,0:T(4,128)S(1)} %get-tuple-element.11.rest_0_, f32[4,128]{1,0:T(4,128)S(1)} %collective-permute-done.rest_1_, f32[4,128]{1,0:T(4,128)S(1)} %collective-permute-done.1.rest_2_, ...), custom_call_target="tpu_custom_call" | custom-call | flops 1073741824 | bytes 2097152 | tf_op jit(solution)/shard_map/pallas_call | solution.py:318
  34.2 12.2 %all_to_all.10.g_ref = bf16[32,32,128]{2,1,0:T(8,128)(2,1)S(1)} all-to-all(bf16[32,32,128]{2,1,0:T(8,128)(2,1)S(1)} %shard_map.47), channel_id=1, replica_groups={{0,1,2,3,8,9,10,11,16,17,18,19,24,25,26,27,4,5,6,7,12,13,14,15,20,21,22..., dimensions={0} | all-to-all | bytes 524288 | tf_op jit(solution)/shard_map/all_to_all | solution.py:274
  46.4 0.8 %shard_map.48 = bf16[64,2048]{1,0:T(8,128)(2,1)} custom-call(bf16[32,32,128]{2,1,0:T(8,128)(2,1)S(1)} %all_to_all.10.g_ref), custom_call_target="tpu_custom_call" | custom-call | flops 262144 | bytes 524288 | tf_op jit(solution)/shard_map/pallas_call | solution.py:336
Async XLA Ops:
  2.2 28.8 %all-to-all-start = ((bf16[32,96,128]{2,1,0:T(8,128)(2,1)}), bf16[32,96,128]{2,1,0:T(8,128)(2,1)S(1)}, u32[]{:S(2)}, u32[]{:S(2)}) async-start(bf16[32,96,128]{2,1,0:T(8,128)(2,1)} %bitcast.2), calls=%async_computation | async-start | bytes 1572864 | tf_op jit(solution)/shard_map/all_to_all | solution.py:274
  9.5 4.6 %collective-permute-start = (f32[4,128]{1,0:T(4,128)S(1)}, f32[4,128]{1,0:T(4,128)S(1)}, u32[]{:S(2)}, u32[]{:S(2)}) collective-permute-start(f32[4,128]{1,0:T(4,128)S(1)} %get-tuple-element.12), channel_id=1, source_target_pairs={{0,1},{1,2},{2,3},{3,0},{4,5},{5,6},{6,7},{7,4},{8,9},{9,10},{10,1... | collective-permute-start | bytes 6152 | tf_op jit(solution)/shard_map/ppermute | solution.py:314
  9.8 5.4 %collective-permute-start.1 = (f32[4,128]{1,0:T(4,128)S(1)}, f32[4,128]{1,0:T(4,128)S(1)}, u32[]{:S(2)}, u32[]{:S(2)}) collective-permute-start(f32[4,128]{1,0:T(4,128)S(1)} %get-tuple-element.13), channel_id=1, source_target_pairs={{0,2},{1,3},{2,0},{3,1},{4,6},{5,7},{6,4},{7,5},{8,10},{9,11},{10,... | collective-permute-start | bytes 6152 | tf_op jit(solution)/shard_map/ppermute | solution.py:314
  11.5 3.8 %collective-permute-start.2 = (f32[4,128]{1,0:T(4,128)S(1)}, f32[4,128]{1,0:T(4,128)S(1)}, u32[]{:S(2)}, u32[]{:S(2)}) collective-permute-start(f32[4,128]{1,0:T(4,128)S(1)} %get-tuple-element.14), channel_id=1, source_target_pairs={{0,3},{1,0},{2,1},{3,2},{4,7},{5,4},{6,5},{7,6},{8,11},{9,8},{10,9... | collective-permute-start | bytes 6152 | tf_op jit(solution)/shard_map/ppermute | solution.py:314
